TPU v7x, 32 devices: a whole 2x2x4 slice. The times are simulated.
32 devices in a mesh: grp: 2 (over x), gz: 8 (over z, y), col: 2 (over core).
Axes of the slice: x: 2, y: 2, z: 4, core: 2. Of those that a mesh axis runs over, the one named last changes fastest.
Arguments:
- noisy_image: float32 [4, 1024, 768], P('grp', 'gz', 'col'), parts along dimension 0, may hold values from -6 to 6
- fresh_noise: float32 [4, 1024, 768], P('grp', 'gz', 'col'), parts along dimension 0, may hold values from -6 to 6
- coil_maps: float32 [8, 4, 1024, 768], P('col', 'grp', 'gz'), parts along dimension 1, may hold values from -1.5 to 1.5
- measured: float32 [4, 768, 8, 1024], P('grp', 'gz', 'col'), parts along dimension 0, may hold values from -2.4 to 2.4
- sampled: int32 [768, 2048], P('gz', 'grp'), parts along dimension 1, may hold values 0 or 1
- first_kernel: bfloat16 [9, 64, 2], replicated, may hold values from -1.5 to 1.5
- inner_kernels: bfloat16 [1, 9, 64, 64], replicated, may hold values from -0.25 to 0.25
- last_kernel: bfloat16 [9, 2, 64], replicated, may hold values from -0.25 to 0.25
Outputs:
- next_image: float32 [4, 1024, 768], P('grp', 'gz', 'col'), parts along dimension 0
There are 2 independent parts, one for each index of `grp`. A program takes and returns all parts, laid end to end along the dimension named above; an argument that names none is the same for every part. Nothing has to cross between parts.
All inputs are finite; a program needn't handle non-finite values. No bound on the sum of `sampled` on one device may be relied on, other than what follows from the above.
Results may differ from a plain program's by a relative error of at most 0.00044.
Values may be sent and summed in bfloat16 or wider, within the bound.
No kernel may reach another device: no remote copies, remote signals or barrier semaphores. Data moves between devices by JAX's collectives and lax.ppermute only.
A program may use at most 128 MiB of HBM per device.

v0:
```python
import math
from functools import partial

import jax
import jax.numpy as jnp
import ml_dtypes
import numpy as np
from jax import lax
from jax.experimental import pallas as pl
from jax.experimental.pallas import tpu as pltpu
from jax.sharding import PartitionSpec as P

SCALE_NOW = 0.8
SIGMA_NOW = 0.6
STEP_GAIN = 1.0
SCALE_NEXT = 0.9
DIRECT_GAIN = 0.31622776601683794
NOISE_GAIN = 0.3

NOISY_MAX = 6.0
MAPS_MAX = 1.5
MEASURED_MAX = 2.4

F32 = jnp.float32
BF16 = jnp.bfloat16
LANES = 128
EDGE = 8
MIB = 1024 * 1024
INNER = 256


def ceil_to(value, step):
    return -(-value // step) * step


def tap_choice(rows, cols):
    choice = np.zeros(rows.shape + (9,), np.float32)
    for index in np.ndindex(rows.shape):
        a, b = rows[index], cols[index]
        if 0 <= a < 3 and 0 <= b < 3:
            choice[index + (3 * a + b,)] = 1.0
    return choice


def tap_choices():
    pair = np.eye(2, dtype=np.float32)
    first, last = [], []
    for c, r in np.ndindex(2, 2):
        s, d, x = np.meshgrid(*map(np.arange, (4, 4, 16)), indexing="ij")
        chosen = tap_choice(x - 5 - 2 * s - r, d - c)
        first.append(np.einsum("sdxt,hk->shdxtk", chosen, pair).reshape(512, 18))
        dr, dc = np.meshgrid(np.arange(4), np.arange(4), indexing="ij")
        chosen = tap_choice(r - dr + 2, c - dc + 2)
        last.append(np.einsum("yxt,hk->yxhtk", chosen, pair).reshape(32, 18))
    middle = []
    for cols, rows in (((0, 1), (0, 1)), ((-1, 2), (0, 1)), ((0, 1), (2, -1)), ((-1, 2), (2, -1))):
        for gamma in cols:
            for rho in rows:
                taps = []
                for c, r in np.ndindex(2, 2):
                    a, b = rho - r + 1, gamma - c + 1
                    taps.append(3 * a + b if 0 <= a < 3 and 0 <= b < 3 else None)
                middle.append(taps)
    return np.stack(first), middle, np.stack(last)


def weights_kernel(cols, height, first_taps, k2, last_taps, choice1, choice3, first, inner, last, scales):
    _, middle, _ = tap_choices()
    ch = k2.shape[1]
    k1 = jnp.concatenate([first_taps[t].astype(F32) for t in range(9)], axis=0).astype(BF16)
    k3 = jnp.concatenate([last_taps[t].astype(F32) for t in range(9)], axis=0).astype(BF16)
    parts = [mm(choice1[i], k1) for i in range(4)]
    first[...] = (0.5 * jnp.concatenate(parts, axis=1)).astype(BF16).reshape(first.shape)
    turned = [(0.5 * jnp.transpose(k2[t].astype(F32))).astype(BF16) for t in range(9)]
    zero = jnp.zeros((ch, ch), BF16)
    for p, taps in enumerate(middle):
        row = [zero if t is None else turned[t] for t in taps]
        inner[p * ch : (p + 1) * ch, :] = jnp.concatenate(row, axis=1)
    parts = [mm(choice3[i], k3) for i in range(4)]
    last[...] = jnp.concatenate(parts, axis=1).astype(BF16)

    def top(value, axes):
        for axis in axes:
            value = jnp.max(value, axis=axis, keepdims=True)
        return value

    gain1 = top(jnp.sum(jnp.abs(k1.astype(F32)), axis=0, keepdims=True), (1,))
    gain2 = sum(jnp.abs(k2[t].astype(F32)) for t in range(9))
    gain2 = top(jnp.sum(gain2, axis=1, keepdims=True), (0,))
    gain3 = jnp.sum(jnp.abs(k3.astype(F32)), axis=1, keepdims=True)
    odd = lax.rem(lax.broadcasted_iota(jnp.int32, gain3.shape, 0), 2) == 1
    gain3 = jnp.maximum(
        jnp.sum(jnp.where(odd, gain3, 0.0), axis=0, keepdims=True),
        jnp.sum(jnp.where(odd, 0.0, gain3), axis=0, keepdims=True),
    )
    predicted = 1.1 * NOISY_MAX * gain1 * gain2 * gain3
    clean = (NOISY_MAX + SIGMA_NOW * predicted) / SCALE_NOW
    spectra = 1.1 * math.sqrt(cols) * 2.0 * MAPS_MAX * clean
    lines = 1.1 * math.sqrt(height) * (spectra + math.sqrt(2.0) * MEASURED_MAX)
    rows = []
    for bound in (spectra, lines):
        rows += [60000.0 / bound, bound / 60000.0]
    scales[...] = jnp.concatenate([jnp.broadcast_to(r, (1, LANES)) for r in rows + rows], axis=0)


def network_weights(first_kernel, inner_kernel, last_kernel, cols, height):
    ch = inner_kernel.shape[1]
    choice1, _, choice3 = tap_choices()
    shapes = ((4, 128, 4 * ch), (16 * ch, 4 * ch), (32, 4 * ch))
    first, inner, last, scales = pl.pallas_call(
        partial(weights_kernel, cols, height),
        out_shape=[jax.ShapeDtypeStruct(d, BF16) for d in shapes]
        + [jax.ShapeDtypeStruct((8, LANES), F32)],
        cost_estimate=pl.CostEstimate(flops=10**7, bytes_accessed=10**6, transcendentals=0),
        compiler_params=pltpu.CompilerParams(vmem_limit_bytes=10 * MIB),
        name="weights",
    )(
        jnp.transpose(first_kernel, (0, 2, 1)),
        inner_kernel,
        last_kernel,
        jnp.asarray(choice1, BF16),
        jnp.asarray(choice3, BF16),
    )
    return (first, inner, last), scales


def split2(value):
    high = value.astype(BF16)
    return high, (value - high.astype(F32)).astype(BF16)


def mm(lhs, rhs):
    return lax.dot_general(lhs, rhs, (((1,), (0,)), ((), ())), preferred_element_type=F32)


def mm_nt(lhs, rhs):
    return lax.dot_general(lhs, rhs, (((1,), (1,)), ((), ())), preferred_element_type=F32)


def network_kernel(
    flags, top, center, bottom, side, first, inner, last, pred, clean, tile, q, hid, hid_side, done, acc
):
    rows, cols = center.shape[1:]
    blocks = rows // 2 + 2
    groups = q.shape[1] // 8 - 1
    used = hid.shape[1]
    step = done.shape[0] // used

    for ch in range(2):
        tile[ch, 0:8, :] = top[ch, :, 0:cols]
        tile[ch, 8 : 8 + rows, :] = center[ch]
        tile[ch, 8 + rows : 16 + rows, :] = bottom[ch, :, 0:cols]
    edge = jnp.concatenate(
        [
            part
            for ch in range(2)
            for part in (top[ch, :, cols:], side[ch], bottom[ch, :, cols:])
        ],
        axis=0,
    ).astype(BF16)
    w = lax.broadcasted_iota(jnp.int32, (cols, 256), 0)
    k = lax.broadcasted_iota(jnp.int32, (cols, 256), 1)
    e = lax.broadcasted_iota(jnp.int32, (EDGE, 256), 0) + jnp.where(flags[2] != 0, cols, -EDGE)
    ke = lax.broadcasted_iota(jnp.int32, (EDGE, 256), 1)
    for d in range(4):
        sel = jnp.where(w == 2 * k - 3 + d, 1.0, 0.0).astype(BF16)
        sel_side = jnp.where(e == 2 * ke - 3 + d, 1.0, 0.0).astype(BF16)
        both = mm(tile[...].reshape(-1, cols).astype(BF16), sel)
        both += mm(edge, sel_side)
        for ch in range(2):
            q[4 * ch + d] = both[ch * (rows + 16) : (ch + 1) * (rows + 16)]

    end = cols // 2 + 1
    tail = end // 8 * 8
    lines = lax.broadcasted_iota(jnp.int32, (8, 256), 0)
    low = jnp.where((lines == 0) & (flags[2] != 0), 0.0, 1.0)
    high = jnp.where((lines == end - tail) & (flags[3] != 0), 0.0, 1.0)

    def silu_rows(half):
        h = half + half * jnp.tanh(half)
        pieces = []
        for start in range(0, h.shape[0], used):
            pieces += [
                h[start : start + 8] * low,
                h[start + 8 : start + tail],
                h[start + tail : start + tail + 8] * high,
            ]
            if tail + 8 < used:
                pieces.append(h[start + tail + 8 : start + used])
        return jnp.concatenate(pieces, axis=0)

    acc[...] = jnp.zeros(acc.shape, F32)
    hid[0] = jnp.zeros(hid.shape[1:], BF16)
    hid_side[0] = jnp.zeros(hid.shape[1:], BF16)

    def first_layer(t, carry):
        window = q[:, pl.ds(pl.multiple_of(8 * t, 8), 16), :].reshape(128, 256)
        window = jnp.transpose(window)[:used].astype(BF16)
        for s in range(4):
            h = silu_rows(mm(window, first[s]))
            place = 4 * t + s + 1
            hid[place] = h.astype(BF16)
            hid_side[place, :, 0:128] = pltpu.roll(h[:, 128:256], 1, 0).astype(BF16)
            hid_side[place, :, 128:256] = pltpu.roll(h[:, 0:128], used - 1, 0).astype(BF16)
        return carry

    lax.fori_loop(0, groups, first_layer, 0)

    for flag, j in ((0, 0), (1, blocks - 1)):

        @pl.when(flags[flag] != 0)
        def _(j=j):
            hid[j + 1] = jnp.zeros(hid.shape[1:], BF16)
            hid_side[j + 1] = jnp.zeros(hid_side.shape[1:], BF16)

    lane = lax.broadcasted_iota(jnp.int32, (step * used, 256), 1)
    below = lax.rem(lane, 128) < 64

    def next_layers(i, carry):
        j = step * i

        def around(ref, offset):
            return ref[pl.ds(j + offset, step)].reshape(step * used, 256)

        lhs = jnp.concatenate(
            [
                around(hid, 1),
                around(hid_side, 1),
                jnp.where(below, around(hid, 2), around(hid, 0)),
                jnp.where(below, around(hid_side, 2), around(hid_side, 0)),
            ],
            axis=1,
        )
        add_parts(j - step)
        done[...] = silu_rows(mm(lhs, inner[...])).astype(BF16)
        return carry

    def add_parts(j):
        for u in range(step):
            part = mm_nt(last[...], done[u * used : (u + 1) * used])
            row = j + u
            gone = ((row == 0) & (flags[0] != 0)) | ((row == blocks - 1) & (flags[1] != 0))
            part = part * jnp.where(gone, 0.0, 1.0)
            where = pl.ds(pl.multiple_of(16 * (row + step), 16), 32)
            for c in range(0, used, 128):
                width = min(128, used - c)
                acc[c // 128, where, 0:width] = acc[c // 128, where, 0:width] + part[:, c : c + width]

    done[...] = jnp.zeros(done.shape, BF16)
    lax.fori_loop(0, blocks // step, next_layers, 0)
    add_parts(blocks - step)

    def pixels(d):
        return jnp.concatenate(
            [
                jnp.concatenate(
                    [
                        acc[c, pl.ds(24 + 16 * step + 2 * d + ch, rows, stride=8), :]
                        for c in range(2)
                    ],
                    axis=1,
                )
                for ch in range(2)
            ],
            axis=0,
        )

    k = lax.broadcasted_iota(jnp.int32, (256, cols), 0)
    w = lax.broadcasted_iota(jnp.int32, (256, cols), 1)
    total = 0.0
    for d, other, shift in ((1, 3, 1), (2, 0, 255)):
        line = pixels(d) + pltpu.roll(pixels(other), shift, 1)
        sel = jnp.where(w == 2 * k - 3 + d, 1.0, 0.0).astype(BF16)
        both = mm(jnp.concatenate(split2(line), axis=0), sel)
        total += both[: 2 * rows] + both[2 * rows :]
    for ch in range(2):
        part = total[ch * rows : (ch + 1) * rows]
        pred[ch] = part
        clean[ch] = (center[ch] - SIGMA_NOW * part) / SCALE_NOW


def run_network(noisy, top, bottom, side, flags, weights):
    _, rows, cols = noisy.shape
    blocks = rows // 2 + 2
    groups = -(-blocks // 4)
    used = ceil_to(cols // 2 + 2, 16)
    step = max(u for u in (1, 2, 3, 6) if blocks % u == 0)
    vmem = pl.BlockSpec(memory_space=pltpu.VMEM)
    shape = jax.ShapeDtypeStruct(noisy.shape, F32)
    return pl.pallas_call(
        network_kernel,
        out_shape=(shape, shape),
        in_specs=[pl.BlockSpec(memory_space=pltpu.SMEM)] + [vmem] * 7,
        out_specs=(vmem, vmem),
        scratch_shapes=[
            pltpu.VMEM((2, rows + 16, cols), F32),
            pltpu.VMEM((8, 8 * groups + 8, 256), F32),
            pltpu.VMEM((4 * groups + 1, used, 256), BF16),
            pltpu.VMEM((4 * groups + 1, used, 256), BF16),
            pltpu.VMEM((step * used, 256), BF16),
            pltpu.VMEM((2, 16 * (blocks + step) + 16, 128), F32),
        ],
        cost_estimate=pl.CostEstimate(
            flops=20 * rows * cols * 64 * 64, bytes_accessed=24 * rows * cols, transcendentals=0
        ),
        compiler_params=pltpu.CompilerParams(vmem_limit_bytes=40 * MIB),
        name="network",
    )(flags, top, noisy, bottom, side, *weights)


def halo(noisy):
    gz = lax.axis_size("gz")
    _, rows, cols = noisy.shape
    left, right = noisy[:, :, :EDGE], noisy[:, :, cols - EDGE :]
    side = swap_cores(jnp.where(lax.axis_index("col") == 0, right, left))
    down = [(i, i + 1) for i in range(gz - 1)]
    lower = jnp.concatenate([noisy[:, rows - EDGE :], side[:, rows - EDGE :]], axis=2)
    upper = jnp.concatenate([noisy[:, :EDGE], side[:, :EDGE]], axis=2)
    top = lax.ppermute(lower, "gz", down)
    bottom = lax.ppermute(upper, "gz", [(b, a) for a, b in down])
    return top, bottom, side


def swap_cores(value):
    assert lax.axis_size("col") == 2
    return lax.ppermute(value, "col", [(0, 1), (1, 0)])


def edge_flags():
    row, col = lax.axis_index("gz"), lax.axis_index("col")
    last_row, last_col = lax.axis_size("gz") - 1, lax.axis_size("col") - 1
    return jnp.stack([row == 0, row == last_row, col == 0, col == last_col]).astype(jnp.int32)


def halves(matrix):
    high = matrix.astype(ml_dtypes.bfloat16)
    low = (matrix - high.astype(np.float64)).astype(ml_dtypes.bfloat16)
    return np.stack([high, low])


def fourier_parts(length, scale):
    index = np.arange(length)
    angle = 2.0 * np.pi * (np.outer(index, index) % length) / length
    return np.cos(angle) * scale, np.sin(angle) * scale


def turn_table(radix, inner):
    angle = 2.0 * np.pi * np.outer(np.arange(radix), np.arange(inner)) / (radix * inner)
    return np.stack([np.cos(angle), np.sin(angle)]).astype(np.float32)


def small_dft(values, sign):
    n = len(values)
    if n == 1:
        return values
    if n % 2 == 0:
        even = small_dft(values[0::2], sign)
        odd = small_dft(values[1::2], sign)
        low, high = [], []
        for q in range(n // 2):
            re, im = times_unit(odd[q], q, n, sign)
            low.append((even[q][0] + re, even[q][1] + im))
            high.append((even[q][0] - re, even[q][1] - im))
        return low + high
    if n == 3:
        (r0, i0), (r1, i1), (r2, i2) = values
        sr, si = r1 + r2, i1 + i2
        half = math.sqrt(3.0) / 2.0 * sign
        dr, di = half * (r1 - r2), half * (i1 - i2)
        tr, ti = r0 - 0.5 * sr, i0 - 0.5 * si
        return [(r0 + sr, i0 + si), (tr - di, ti + dr), (tr + di, ti - dr)]
    out = []
    for q in range(n):
        terms = [times_unit(v, a * q, n, sign) for a, v in enumerate(values)]
        out.append((sum(t[0] for t in terms), sum(t[1] for t in terms)))
    return out


def times_unit(value, power, n, sign):
    re, im = value
    power %= n
    if power == 0:
        return re, im
    if 4 * power == n:
        return (-im, re) if sign > 0 else (im, -re)
    if 2 * power == n:
        return -re, -im
    if 4 * power == 3 * n:
        return (im, -re) if sign > 0 else (-im, re)
    c = math.cos(2.0 * math.pi * power / n)
    s = sign * math.sin(2.0 * math.pi * power / n)
    return c * re - s * im, c * im + s * re


def turn(value, cos, sin, sign):
    re, im = value
    if sign > 0:
        return re * cos - im * sin, im * cos + re * sin
    return re * cos + im * sin, im * cos - re * sin


def beside(parts, axis):
    return jnp.concatenate([parts[0], parts[0], parts[1]], axis=axis)


def against(matrix, axis):
    return jnp.concatenate([matrix[0], matrix[1], matrix[0]], axis=axis)


def columns_forward_kernel(first, mine, other, maps, scales, matrix, table, out):
    radix, inner = table.shape[1:]
    coils = maps.shape[0]
    rows, _ = mine.shape[1:]
    groups = out.shape[0]
    per = inner // groups
    lead, me = first[0] != 0, first[1]
    image = [
        jnp.concatenate(
            [jnp.where(lead, mine[p], other[p]), jnp.where(lead, other[p], mine[p])], axis=1
        )
        * scales[0:1, 0:1]
        for p in range(2)
    ]
    turned = []
    for coil in range(coils):
        maps_real, maps_imag = maps[coil, 0], maps[coil, 1]
        coil_image = (
            maps_real * image[0] - maps_imag * image[1],
            maps_real * image[1] + maps_imag * image[0],
        )
        parts = [
            tuple(v[:, a * inner : (a + 1) * inner] for v in coil_image) for a in range(radix)
        ]
        parts = small_dft(parts, -1)
        turned.append(
            [
                turn(part, table[0, q : q + 1, :], table[1, q : q + 1, :], -1) if q else part
                for q, part in enumerate(parts)
            ]
        )
    for q in range(radix):
        data = jnp.concatenate([jnp.concatenate(turned[c][q], axis=1) for c in range(coils)], axis=0)
        result = mm_nt(against(matrix, 1), beside(split2(data), 1))
        for p in range(2):
            for g in range(groups):
                start = p * inner + g * per
                for c in range(coils):
                    out[lax.bitwise_xor(g, me), p, c, q] = result[start : start + per, c * rows : (c + 1) * rows]


def columns_forward(first, mine, other, maps, scales, groups, chunk, chunks):
    coils, _, rows, cols = maps.shape
    coils //= chunks
    inner = INNER
    radix = cols // inner
    c, s = fourier_parts(inner, 1.0 / math.sqrt(cols))
    matrix = halves(np.block([[c, s], [-s, c]]))
    table = turn_table(radix, inner)
    vmem = pl.BlockSpec(memory_space=pltpu.VMEM)
    per = inner // groups
    return pl.pallas_call(
        columns_forward_kernel,
        out_shape=jax.ShapeDtypeStruct((groups, 2, coils, radix, per, rows), F32),
        grid=(1,),
        in_specs=[
            pl.BlockSpec(memory_space=pltpu.SMEM),
            vmem,
            vmem,
            pl.BlockSpec((coils, 2, rows, cols), lambda i: (chunk, 0, 0, 0)),
            vmem,
            vmem,
            vmem,
        ],
        out_specs=pl.BlockSpec(
            (groups, 2, coils, radix, per, rows), lambda i: (0, 0, 0, 0, 0, 0)
        ),
        cost_estimate=pl.CostEstimate(
            flops=24 * coils * rows * cols * inner,
            bytes_accessed=16 * coils * rows * cols,
            transcendentals=0,
        ),
        compiler_params=pltpu.CompilerParams(vmem_limit_bytes=20 * MIB),
        name="columns_forward",
    )(first, mine, other, maps, scales, jnp.asarray(matrix), jnp.asarray(table))


def rows_kernel(place, data, kept, target, scales, forward, inverse, table, out, lines):
    radix = table.shape[1]
    count = data.shape[2]
    spots = [lax.bitwise_xor(a, place[1]) for a in range(radix)]
    parts = small_dft([(data[spot, 0], data[spot, 1]) for spot in spots], -1)
    for q, part in enumerate(parts):
        if q:
            part = turn(part, table[0, q : q + 1, :], table[1, q : q + 1, :], -1)
        for p in range(2):
            lines[q * count : (q + 1) * count, p * LANES : (p + 1) * LANES] = part[p]
    spectrum = mm(beside(split2(lines[...]), 1), against(forward, 0))
    keep = kept[...].reshape(radix * count, LANES) * scales[2:3, :]
    unit = scales[1:2, :]
    residual = jnp.concatenate(
        [
            keep
            * (spectrum[:, p * LANES : (p + 1) * LANES] * unit - target[p].reshape(-1, LANES))
            for p in range(2)
        ],
        axis=1,
    )
    lines[...] = mm(beside(split2(residual), 1), against(inverse, 0))
    back = []
    for q in range(radix):
        part = tuple(
            lines[q * count : (q + 1) * count, p * LANES : (p + 1) * LANES] for p in range(2)
        )
        if q:
            part = turn(part, table[0, q : q + 1, :], table[1, q : q + 1, :], 1)
        back.append(part)
    for spot, (re, im) in zip(spots, small_dft(back, 1)):
        out[spot, 0] = re
        out[spot, 1] = im


def rows_both_ways(place, data, kept, target, scales, first_line):
    radix, _, count, _ = data.shape
    pencil = kept.shape[1]
    c, s = fourier_parts(LANES, 1.0 / math.sqrt(radix * LANES))
    forward = halves(np.block([[c, -s], [s, c]]))
    inverse = halves(np.block([[c, s], [-s, c]]))
    table = turn_table(radix, LANES)
    block = max(b for b in range(8, 56, 8) if pencil % b == 0)
    offset, repeat = first_line // block, pencil // block
    vmem = pl.BlockSpec(memory_space=pltpu.VMEM)
    spec = pl.BlockSpec((radix, 2, block, LANES), lambda i: (0, 0, i, 0))
    return pl.pallas_call(
        rows_kernel,
        out_shape=jax.ShapeDtypeStruct(data.shape, F32),
        grid=(count // block,),
        in_specs=[
            pl.BlockSpec(memory_space=pltpu.SMEM),
            spec,
            pl.BlockSpec((radix, block, LANES), lambda i: (0, lax.rem(i + offset, repeat), 0)),
            pl.BlockSpec((2, radix, block, LANES), lambda i: (0, 0, i + offset, 0)),
            vmem,
            vmem,
            vmem,
            vmem,
        ],
        out_specs=spec,
        scratch_shapes=[pltpu.VMEM((radix * block, 2 * LANES), F32)],
        cost_estimate=pl.CostEstimate(
            flops=24 * radix * count * LANES * LANES,
            bytes_accessed=32 * radix * count * LANES,
            transcendentals=0,
        ),
        compiler_params=pltpu.CompilerParams(vmem_limit_bytes=12 * MIB),
        name="rows_both_ways",
    )(place, data, kept, target, scales, jnp.asarray(forward), jnp.asarray(inverse), jnp.asarray(table))


def columns_inverse_kernel(last, first, data, maps, scales, matrix, table, *refs):
    radix, inner = table.shape[1:]
    groups = data.shape[0]
    coils, _, rows, cols = maps.shape
    base, outs = (None, refs) if len(refs) == 1 else (refs[0], refs[1:])
    parts = []
    for q in range(radix):
        lines = jnp.concatenate(
            [
                jnp.transpose(
                    jnp.concatenate(
                        [
                            data[lax.bitwise_xor(g, first[1]), p, c, q]
                            for p in range(2)
                            for g in range(groups)
                        ], axis=0
                    )
                )
                for c in range(coils)
            ],
            axis=0,
        )
        result = mm(beside(split2(lines), 1), against(matrix, 0))
        part = (result[:, :inner], result[:, inner:])
        if q:
            part = turn(part, table[0, q : q + 1, :], table[1, q : q + 1, :], 1)
        parts.append(part)
    sums = [[], []]
    for a, (re, im) in enumerate(small_dft(parts, 1)):
        where = slice(a * inner, (a + 1) * inner)
        total = [0.0, 0.0]
        for c in range(coils):
            maps_real, maps_imag = maps[c, 0, :, where], maps[c, 1, :, where]
            x, y = re[c * rows : (c + 1) * rows], im[c * rows : (c + 1) * rows]
            total[0] += maps_real * x + maps_imag * y
            total[1] += maps_real * y - maps_imag * x
        for p in range(2):
            part = total[p] * scales[3:4, 0:1]
            sums[p].append(part if base is None else base[p, :, where] + part)
    lead = first[0] != 0
    for p in range(2):
        line = jnp.concatenate(sums[p], axis=1)
        if last:
            own, away = line[:, : cols // 2], line[:, cols // 2 :]
            outs[0][p] = jnp.where(lead, own, away)
            outs[1][p] = jnp.where(lead, away, own)
        else:
            outs[0][p] = line


def columns_inverse(first, data, maps, scales, chunk, chunks, base):
    _, _, coils, radix, _, rows = data.shape
    cols = maps.shape[3]
    inner = cols // radix
    c, s = fourier_parts(inner, 1.0 / math.sqrt(cols))
    matrix = halves(np.block([[c, s], [-s, c]]))
    table = turn_table(radix, inner)
    vmem = pl.BlockSpec(memory_space=pltpu.VMEM)
    last = chunk == chunks - 1
    if last:
        shape = [jax.ShapeDtypeStruct((2, rows, cols // 2), F32)] * 2
    else:
        shape = [jax.ShapeDtypeStruct((2, rows, cols), F32)]
    return pl.pallas_call(
        partial(columns_inverse_kernel, last),
        out_shape=shape,
        grid=(1,),
        in_specs=[
            pl.BlockSpec(memory_space=pltpu.SMEM),
            vmem,
            pl.BlockSpec((coils, 2, rows, cols), lambda i: (chunk, 0, 0, 0)),
            vmem,
            vmem,
            vmem,
        ]
        + [vmem] * len(base),
        out_specs=[vmem] * len(shape),
        cost_estimate=pl.CostEstimate(
            flops=24 * coils * rows * cols * inner,
            bytes_accessed=16 * coils * rows * cols,
            transcendentals=0,
        ),
        compiler_params=pltpu.CompilerParams(vmem_limit_bytes=20 * MIB),
        name="columns_inverse",
    )(first, data, maps, scales, jnp.asarray(matrix), jnp.asarray(table), *base)


def target_kernel(radix3, token, *refs):
    tiles = (len(refs) - 4) // 2
    measured, sampled = refs[:tiles], refs[tiles : 2 * tiles]
    target, kept, lines, order = refs[2 * tiles :]
    radix, pencil, _ = kept.shape
    count, height = lines.shape
    coils = count // pencil
    per = pencil // radix3

    @pl.when(pl.program_id(0) == 0)
    def _():
        source = lax.broadcasted_iota(jnp.int32, (height, LANES), 0)
        place = lax.broadcasted_iota(jnp.int32, (height, LANES), 1)
        for q in range(radix):
            order[:, q * LANES : (q + 1) * LANES] = jnp.where(
                source == radix * place + q, 1.0, 0.0
            ).astype(BF16)
        for t in range(tiles):
            for q in range(radix3):
                lines[q * per : (q + 1) * per, t * LANES : (t + 1) * LANES] = sampled[t][
                    pl.ds(q, per, stride=radix3), :
                ].astype(F32)
        picked = mm(lines[0:pencil, :].astype(BF16), order[...])
        for q in range(radix):
            kept[q] = picked[:, q * LANES : (q + 1) * LANES]

    for t in range(tiles):
        source = measured[t].reshape(count, LANES)
        for c in range(coils):
            for q in range(radix3):
                start = c * pencil + q * per
                lines[start : start + per, t * LANES : (t + 1) * LANES] = source[
                    pl.ds(q * coils + c, per, stride=radix3 * coils), :
                ]
    high, low = split2(lines[...])
    for q in range(0, radix, 2):
        width = min(2, radix - q) * LANES
        part = order[:, q * LANES : q * LANES + width]
        picked = mm(high, part) + mm(low, part)
        for k in range(0, width, LANES):
            target[0, q + k // LANES] = picked[:, k : k + LANES]


def prepare_target(token, measured, sampled, radix3):
    _, pencil, coils, height = measured.shape
    radix = height // LANES
    count = pencil * coils
    return pl.pallas_call(
        partial(target_kernel, radix3),
        out_shape=(
            jax.ShapeDtypeStruct((2, radix, count, LANES), F32),
            jax.ShapeDtypeStruct((radix, pencil, LANES), F32),
        ),
        grid=(2,),
        in_specs=[pl.BlockSpec(memory_space=pltpu.SMEM)]
        + [
            pl.BlockSpec((1, pencil, coils, LANES), lambda i, t=t: (i, 0, 0, t))
            for t in range(radix)
        ]
        + [pl.BlockSpec((pencil, LANES), lambda i, t=t: (0, t)) for t in range(radix)],
        out_specs=(
            pl.BlockSpec((1, radix, count, LANES), lambda i: (i, 0, 0, 0)),
            pl.BlockSpec((radix, pencil, LANES), lambda i: (0, 0, 0)),
        ),
        scratch_shapes=[pltpu.VMEM((count, height), F32), pltpu.VMEM((height, height), BF16)],
        cost_estimate=pl.CostEstimate(
            flops=8 * count * height * height, bytes_accessed=16 * count * height, transcendentals=0
        ),
        compiler_params=pltpu.CompilerParams(vmem_limit_bytes=20 * MIB),
        name="target",
    )(token, *[measured] * radix, *[sampled] * radix)


def pairwise(groups):
    return groups <= 8 and groups & (groups - 1) == 0


def send(value):
    groups = value.shape[0]
    if not pairwise(groups):
        value = value.astype(jnp.float16)
        return [lax.all_to_all(value, "gz", split_axis=0, concat_axis=0, tiled=True)]
    return [value[0]] + [
        lax.ppermute(value[k].astype(jnp.float16), "gz", [(i, i ^ k) for i in range(groups)])
        for k in range(1, groups)
    ]


def receive(parts):
    if len(parts) == 1:
        return parts[0].astype(F32)
    return jnp.stack([part.astype(F32) for part in parts])


def after(value, *earlier):
    return lax.optimization_barrier((value, *earlier))[0]


def local(
    noisy_image, fresh_noise, coil_maps, measured, sampled, first_kernel, inner_kernels, last_kernel
):
    groups = lax.axis_size("gz")
    coils, _, rows, cols = coil_maps.shape
    height = measured.shape[3]
    radix, inner = cols // INNER, INNER
    per = inner // groups
    row_radix = height // LANES
    chunks = 2
    pencil = radix * per
    count = coils * pencil // chunks
    place = lax.axis_index("gz") if pairwise(groups) else 0
    lead = jnp.stack([lax.axis_index("col") == 0, place]).astype(jnp.int32)

    weights, scales = network_weights(
        first_kernel, inner_kernels[0], last_kernel, cols, height
    )
    top, bottom, side = halo(noisy_image)
    predicted, clean = run_network(noisy_image, top, bottom, side, edge_flags(), weights)
    other = swap_cores(clean)

    token = lead
    arrived = []
    for chunk in range(chunks):
        spectra = columns_forward(token, clean, other, coil_maps, scales, groups, chunk, chunks)
        spectra = send(spectra.reshape(groups, 2, count, rows))
        token = after(lead, spectra[0])
        arrived.append(spectra)
    target, kept = prepare_target(token, measured, sampled, radix)

    back = []
    for chunk in range(chunks):
        lines = receive(after(arrived[chunk], token))
        if rows != LANES:
            lines = jnp.transpose(lines, (1, 2, 0, 3)).reshape(2, -1, row_radix, LANES)
            lines = jnp.transpose(lines, (2, 0, 1, 3))
        lines = rows_both_ways(lead, lines, kept, target, scales, chunk * (coils // chunks) * pencil)
        if rows != LANES:
            lines = jnp.transpose(lines, (1, 2, 0, 3)).reshape(2, -1, groups, rows)
            lines = jnp.transpose(lines, (2, 0, 1, 3))
        token = lines[0]
        back.append(send(lines))

    gradient = []
    for chunk in range(chunks):
        lines = receive(after(back[chunk], *gradient))
        lines = lines.reshape(groups, 2, coils // chunks, radix, per, rows)
        gradient = columns_inverse(lead, lines, coil_maps, scales, chunk, chunks, gradient)

    own, away = gradient
    own = own + swap_cores(away)
    update = clean - STEP_GAIN * own
    return SCALE_NEXT * update + DIRECT_GAIN * predicted + NOISE_GAIN * fresh_noise


def solution(mesh):
    in_specs = (
        P("grp", "gz", "col"),
        P("grp", "gz", "col"),
        P("col", "grp", "gz", None),
        P("grp", "gz", "col", None),
        P("gz", "grp"),
        P(),
        P(),
        P(),
    )
    out_specs = P("grp", "gz", "col")

    return jax.shard_map(local, mesh=mesh, in_specs=in_specs, out_specs=out_specs, check_vma=False)
```

profile of v0, /device:TPU:0, one launch (start us, length us, event | category | flops | bytes accessed | tf_op | source)
XLA Modules:
  0.0 128.5 jit_solution(16870999968307369783)
XLA Ops:
  0.0 1.1 slice_select_fusion
  1.1 0.6 collective-permute-start
  1.6 0.8 fusion.2
  2.4 0.2 collective-permute-done.side
  2.6 4.8 %collective-permute-start.1 = (f32[2,8,392]{2,1,0:T(8,128)S(1)}, f32[2,8,392]{2,1,0:T(8,128)S(1)}, u32[]{:S(2)}, u32[]{:S(2)}) collective-permute-start(f32[2,8,392]{2,1,0:T(8,128)S(1)} %pad_maximum_fusion), channel_id=1, source_target_pairs={{0,2},{2,4},{4,6},{6,8},{8,10},{10,12},{12,14},{1,3},{3,5},{5,7},{... | collective-permute-start | bytes 75272 | tf_op jit(solution)/shard_map/ppermute | solution.py:319
  7.4 1.3 %collective-permute-start.2 = (f32[2,8,392]{2,1,0:T(8,128)S(1)}, f32[2,8,392]{2,1,0:T(8,128)S(1)}, u32[]{:S(2)}, u32[]{:S(2)}) collective-permute-start(f32[2,8,392]{2,1,0:T(8,128)S(1)} %pad_maximum_fusion.1), channel_id=1, source_target_pairs={{2,0},{4,2},{6,4},{8,6},{10,8},{12,10},{14,12},{3,1},{5,3},{7,5},{... | collective-permute-start | bytes 75272 | tf_op jit(solution)/shard_map/ppermute | solution.py:320
  8.8 1.0 copy-done.8
  9.8 0.9 copy-done.10
  10.8 0.8 copy-done.12
  11.5 0.7 copy-done.14
  12.2 0.7 copy-done.15
  12.9 0.4 weights.1
  13.3 1.0 copy-done.9
  14.3 20.7 %network.1 = (f32[2,128,384]{2,1,0:T(8,128)S(1)}, f32[2,128,384]{2,1,0:T(8,128)S(1)}) custom-call(s32[4]{0:T(128)S(1)} %add_convert_fusion.flags, f32[2,8,392]{2,1,0:T(8,128)S(1)} %collective-permute-done.1.top, f32[2,128,384]{2,1,0:T(8,128)S(1)} %copy-done.9, f32[2,8,392]{2,1,0:T(8,128)S(1)} %collective-permute-done.2.bottom, ...), custom_call_target="tpu_custom_call" | custom-call | flops 4026531840 | bytes 1179648 | tf_op jit(solution)/shard_map/network/pallas_call | solution.py:290
  35.2 1.6 %collective-permute-done.3.other = f32[2,128,384]{2,1,0:T(8,128)S(1)} collective-permute-done((f32[2,128,384]{2,1,0:T(8,128)S(1)}, f32[2,128,384]{2,1,0:T(8,128)S(1)}, u32[]{:S(2)}, u32[]{:S(2)}) %collective-permute-start.3) | collective-permute-done | bytes 393248 | tf_op jit(solution)/shard_map/ppermute | solution.py:326
  36.8 2.4 %columns_forward.2 = f32[8,2,2,3,32,128]{5,4,3,2,1,0:T(8,128)S(1)} custom-call(s32[2]{0:T(128)S(1)} %pad_add_fusion.first.token.place, f32[2,128,384]{2,1,0:T(8,128)S(1)} %get-tuple-element.52.mine, f32[2,128,384]{2,1,0:T(8,128)S(1)} %collective-permute-done.3.other, f32[4,2,128,768]{3,2,1,0:T(8,128)S(1)} %copy-done.1, ...), custom_call_target="tpu_custom_call" | custom-call | flops 1207959552 | bytes 3145728 | tf_op jit(solution)/shard_map/columns_forward/pallas_call | solution.py:461
  39.3 0.2 convert.66
  39.5 2.4 %columns_forward.3 = f32[8,2,2,3,32,128]{5,4,3,2,1,0:T(8,128)S(1)} custom-call(s32[2]{0:T(128)S(1)} %pad_add_fusion.first.token.place, f32[2,128,384]{2,1,0:T(8,128)S(1)} %get-tuple-element.52.mine, f32[2,128,384]{2,1,0:T(8,128)S(1)} %collective-permute-done.3.other, f32[4,2,128,768]{3,2,1,0:T(8,128)S(1)} %copy-done.1, ...), custom_call_target="tpu_custom_call" | custom-call | flops 1207959552 | bytes 3145728 | tf_op jit(solution)/shard_map/columns_forward/pallas_call | solution.py:461
  42.0 0.2 convert.65
  42.2 0.2 fusion
  42.3 0.8 copy-done.4
  43.1 5.6 %collective-permute-start.16 = (f16[2,192,128]{2,1,0:T(8,128)(2,1)S(1)}, f16[2,192,128]{2,1,0:T(8,128)(2,1)S(1)}, u32[]{:S(2)}, u32[]{:S(2)}) collective-permute-start(f16[2,192,128]{2,1,0:T(8,128)(2,1)S(1)} %bitcast.164), channel_id=1, source_target_pairs={{0,12},{2,14},{4,8},{6,10},{8,4},{10,6},{12,0},{14,2},{1,13},{3,15... | collective-permute-start | bytes 294920 | tf_op jit(solution)/shard_map/ppermute | solution.py:729
  48.7 0.3 collective-permute-start.17
  49.0 1.6 %collective-permute-start.15 = (f16[2,192,128]{2,1,0:T(8,128)(2,1)S(1)}, f16[2,192,128]{2,1,0:T(8,128)(2,1)S(1)}, u32[]{:S(2)}, u32[]{:S(2)}) collective-permute-start(f16[2,192,128]{2,1,0:T(8,128)(2,1)S(1)} %bitcast.162), channel_id=1, source_target_pairs={{0,10},{2,8},{4,14},{6,12},{8,2},{10,0},{12,6},{14,4},{1,11},{3,9}... | collective-permute-start | bytes 294920 | tf_op jit(solution)/shard_map/ppermute | solution.py:729
  50.7 1.9 %collective-permute-start.14 = (f16[2,192,128]{2,1,0:T(8,128)(2,1)S(1)}, f16[2,192,128]{2,1,0:T(8,128)(2,1)S(1)}, u32[]{:S(2)}, u32[]{:S(2)}) collective-permute-start(f16[2,192,128]{2,1,0:T(8,128)(2,1)S(1)} %bitcast.161), channel_id=1, source_target_pairs={{0,8},{2,10},{4,12},{6,14},{8,0},{10,2},{12,4},{14,6},{1,9},{3,11}... | collective-permute-start | bytes 294920 | tf_op jit(solution)/shard_map/ppermute | solution.py:729
  52.6 1.5 %collective-permute-start.13 = (f16[2,192,128]{2,1,0:T(8,128)(2,1)S(1)}, f16[2,192,128]{2,1,0:T(8,128)(2,1)S(1)}, u32[]{:S(2)}, u32[]{:S(2)}) collective-permute-start(f16[2,192,128]{2,1,0:T(8,128)(2,1)S(1)} %bitcast.160), channel_id=1, source_target_pairs={{0,6},{2,4},{4,2},{6,0},{8,14},{10,12},{12,10},{14,8},{1,7},{3,5},... | collective-permute-start | bytes 294920 | tf_op jit(solution)/shard_map/ppermute | solution.py:729
  54.1 5.7 %target.1 = (f32[2,8,384,128]{3,2,1,0:T(8,128)S(1)}, f32[8,96,128]{2,1,0:T(8,128)S(1)}) custom-call(s32[2]{0:T(128)S(1)} %pad_add_fusion.first.token.place, f32[2,96,4,1024]{3,2,1,0:T(4,128)S(1)} %copy-done, f32[2,96,4,1024]{3,2,1,0:T(4,128)S(1)} %copy-done, f32[2,96,4,1024]{3,2,1,0:T(4,128)S(1)} %copy-done, f32[2,96,4,1024]{3,2,1,0:T(4,128)S(1)} %copy-done, ...), custom_call_target="tpu_custom_call" | custom-call | flops 3221225472 | bytes 6291456 | tf_op jit(solution)/shard_map/target/pallas_call | solution.py:693
  59.8 0.8 collective-permute-start.12
  60.7 1.2 collective-permute-start.11
  61.9 0.1 fusion.1
  62.0 2.6 %collective-permute-done.15 = f16[2,192,128]{2,1,0:T(8,128)(2,1)S(1)} collective-permute-done((f16[2,192,128]{2,1,0:T(8,128)(2,1)S(1)}, f16[2,192,128]{2,1,0:T(8,128)(2,1)S(1)}, u32[]{:S(2)}, u32[]{:S(2)}) %collective-permute-start.15) | collective-permute-done | bytes 98336 | tf_op jit(solution)/shard_map/ppermute | solution.py:729
  64.6 2.5 %collective-permute-start.9 = (f16[2,192,128]{2,1,0:T(8,128)(2,1)S(1)}, f16[2,192,128]{2,1,0:T(8,128)(2,1)S(1)}, u32[]{:S(2)}, u32[]{:S(2)}) collective-permute-start(f16[2,192,128]{2,1,0:T(8,128)(2,1)S(1)} %bitcast.157), channel_id=1, source_target_pairs={{0,12},{2,14},{4,8},{6,10},{8,4},{10,6},{12,0},{14,2},{1,13},{3,15... | collective-permute-start | bytes 294920 | tf_op jit(solution)/shard_map/ppermute | solution.py:729
  67.1 2.2 %collective-permute-start.10 = (f16[2,192,128]{2,1,0:T(8,128)(2,1)S(1)}, f16[2,192,128]{2,1,0:T(8,128)(2,1)S(1)}, u32[]{:S(2)}, u32[]{:S(2)}) collective-permute-start(f16[2,192,128]{2,1,0:T(8,128)(2,1)S(1)} %bitcast.156), channel_id=1, source_target_pairs={{0,14},{2,12},{4,10},{6,8},{8,6},{10,4},{12,2},{14,0},{1,15},{3,13... | collective-permute-start | bytes 294920 | tf_op jit(solution)/shard_map/ppermute | solution.py:729
  69.3 3.5 %collective-permute-start.7 = (f16[2,192,128]{2,1,0:T(8,128)(2,1)S(1)}, f16[2,192,128]{2,1,0:T(8,128)(2,1)S(1)}, u32[]{:S(2)}, u32[]{:S(2)}) collective-permute-start(f16[2,192,128]{2,1,0:T(8,128)(2,1)S(1)} %bitcast.154), channel_id=1, source_target_pairs={{0,8},{2,10},{4,12},{6,14},{8,0},{10,2},{12,4},{14,6},{1,9},{3,11}... | collective-permute-start | bytes 294920 | tf_op jit(solution)/shard_map/ppermute | solution.py:729
  72.8 0.5 collective-permute-start.6
  73.5 4.4 %rows_both_ways.2 = f32[8,2,192,128]{3,2,1,0:T(8,128)S(1)} custom-call(s32[2]{0:T(128)S(1)} %pad_add_fusion.first.token.place, f32[8,2,192,128]{3,2,1,0:T(8,128)S(1)} %convert_dynamic-update-slice_fusion.21.data, f32[8,96,128]{2,1,0:T(8,128)S(1)} %get-tuple-element.64.kept, f32[2,8,384,128]{3,2,1,0:T(8,128)S(1)} %get-tuple-element.65.target, ...), custom_call_target="tpu_custom_call" | custom-call | flops 603979776 | bytes 6291456 | tf_op jit(solution)/shard_map/rows_both_ways/pallas_call | solution.py:533
  77.9 0.2 convert.68
  78.1 0.2 slice_bitcast_fusion.2
  78.3 1.9 %collective-permute-start.5 = (f16[2,192,128]{2,1,0:T(8,128)(2,1)S(1)}, f16[2,192,128]{2,1,0:T(8,128)(2,1)S(1)}, u32[]{:S(2)}, u32[]{:S(2)}) collective-permute-start(f16[2,192,128]{2,1,0:T(8,128)(2,1)S(1)} %bitcast.152), channel_id=1, source_target_pairs={{0,4},{2,6},{4,0},{6,2},{8,12},{10,14},{12,8},{14,10},{1,5},{3,7},... | collective-permute-start | bytes 294920 | tf_op jit(solution)/shard_map/ppermute | solution.py:729
  80.2 1.2 collective-permute-start.4
  81.4 1.1 collective-permute-done.8
  82.5 0.2 collective-permute-done.7
  82.7 1.3 %collective-permute-done.5 = f16[2,192,128]{2,1,0:T(8,128)(2,1)S(1)} collective-permute-done((f16[2,192,128]{2,1,0:T(8,128)(2,1)S(1)}, f16[2,192,128]{2,1,0:T(8,128)(2,1)S(1)}, u32[]{:S(2)}, u32[]{:S(2)}) %collective-permute-start.5) | collective-permute-done | bytes 98336 | tf_op jit(solution)/shard_map/ppermute | solution.py:729
  84.0 0.8 collective-permute-done.4
  84.8 2.5 %collective-permute-start.31 = (f16[2,192,128]{2,1,0:T(8,128)(2,1)S(1)}, f16[2,192,128]{2,1,0:T(8,128)(2,1)S(1)}, u32[]{:S(2)}, u32[]{:S(2)}) collective-permute-start(f16[2,192,128]{2,1,0:T(8,128)(2,1)S(1)} %get-tuple-element.93), channel_id=1, source_target_pairs={{0,14},{2,12},{4,10},{6,8},{8,6},{10,4},{12,2},{14,0},{1,15},{3,13... | collective-permute-start | bytes 294920 | tf_op jit(solution)/shard_map/ppermute | solution.py:729
  87.4 1.9 %collective-permute-start.30 = (f16[2,192,128]{2,1,0:T(8,128)(2,1)S(1)}, f16[2,192,128]{2,1,0:T(8,128)(2,1)S(1)}, u32[]{:S(2)}, u32[]{:S(2)}) collective-permute-start(f16[2,192,128]{2,1,0:T(8,128)(2,1)S(1)} %get-tuple-element.94), channel_id=1, source_target_pairs={{0,12},{2,14},{4,8},{6,10},{8,4},{10,6},{12,0},{14,2},{1,13},{3,15... | collective-permute-start | bytes 294920 | tf_op jit(solution)/shard_map/ppermute | solution.py:729
  89.2 3.2 %collective-permute-start.28 = (f16[2,192,128]{2,1,0:T(8,128)(2,1)S(1)}, f16[2,192,128]{2,1,0:T(8,128)(2,1)S(1)}, u32[]{:S(2)}, u32[]{:S(2)}) collective-permute-start(f16[2,192,128]{2,1,0:T(8,128)(2,1)S(1)} %get-tuple-element.96), channel_id=1, source_target_pairs={{0,8},{2,10},{4,12},{6,14},{8,0},{10,2},{12,4},{14,6},{1,9},{3,11}... | collective-permute-start | bytes 294920 | tf_op jit(solution)/shard_map/ppermute | solution.py:729
  92.5 0.2 collective-permute-start.27
  92.8 4.6 %rows_both_ways.3 = f32[8,2,192,128]{3,2,1,0:T(8,128)S(1)} custom-call(s32[2]{0:T(128)S(1)} %pad_add_fusion.first.token.place, f32[8,2,192,128]{3,2,1,0:T(8,128)S(1)} %convert_dynamic-update-slice_fusion.14.data, f32[8,96,128]{2,1,0:T(8,128)S(1)} %get-tuple-element.64.kept, f32[2,8,384,128]{3,2,1,0:T(8,128)S(1)} %get-tuple-element.65.target, ...), custom_call_target="tpu_custom_call" | custom-call | flops 603979776 | bytes 6291456 | tf_op jit(solution)/shard_map/rows_both_ways/pallas_call | solution.py:533
  97.4 0.2 convert.67
  97.6 0.1 slice_bitcast_fusion.9
  97.8 2.5 %collective-permute-start.26 = (f16[2,192,128]{2,1,0:T(8,128)(2,1)S(1)}, f16[2,192,128]{2,1,0:T(8,128)(2,1)S(1)}, u32[]{:S(2)}, u32[]{:S(2)}) collective-permute-start(f16[2,192,128]{2,1,0:T(8,128)(2,1)S(1)} %get-tuple-element.98), channel_id=1, source_target_pairs={{0,4},{2,6},{4,0},{6,2},{8,12},{10,14},{12,8},{14,10},{1,5},{3,7},... | collective-permute-start | bytes 294920 | tf_op jit(solution)/shard_map/ppermute | solution.py:729
  100.3 1.3 %collective-permute-start.25 = (f16[2,192,128]{2,1,0:T(8,128)(2,1)S(1)}, f16[2,192,128]{2,1,0:T(8,128)(2,1)S(1)}, u32[]{:S(2)}, u32[]{:S(2)}) collective-permute-start(f16[2,192,128]{2,1,0:T(8,128)(2,1)S(1)} %get-tuple-element.99), channel_id=1, source_target_pairs={{0,2},{2,0},{4,6},{6,4},{8,10},{10,8},{12,14},{14,12},{1,3},{3,1},... | collective-permute-start | bytes 294920 | tf_op jit(solution)/shard_map/ppermute | solution.py:729
  101.6 1.4 %collective-permute-done.29 = f16[2,192,128]{2,1,0:T(8,128)(2,1)S(1)} collective-permute-done((f16[2,192,128]{2,1,0:T(8,128)(2,1)S(1)}, f16[2,192,128]{2,1,0:T(8,128)(2,1)S(1)}, u32[]{:S(2)}, u32[]{:S(2)}) %collective-permute-start.29) | collective-permute-done | bytes 98336 | tf_op jit(solution)/shard_map/ppermute | solution.py:729
  103.0 3.8 %collective-permute-start.24 = (f16[2,192,128]{2,1,0:T(8,128)(2,1)S(1)}, f16[2,192,128]{2,1,0:T(8,128)(2,1)S(1)}, u32[]{:S(2)}, u32[]{:S(2)}) collective-permute-start(f16[2,192,128]{2,1,0:T(8,128)(2,1)S(1)} %get-tuple-element.100), channel_id=1, source_target_pairs={{0,14},{2,12},{4,10},{6,8},{8,6},{10,4},{12,2},{14,0},{1,15},{3,13... | collective-permute-start | bytes 294920 | tf_op jit(solution)/shard_map/ppermute | solution.py:729
  106.8 5.6 %collective-permute-start.23 = (f16[2,192,128]{2,1,0:T(8,128)(2,1)S(1)}, f16[2,192,128]{2,1,0:T(8,128)(2,1)S(1)}, u32[]{:S(2)}, u32[]{:S(2)}) collective-permute-start(f16[2,192,128]{2,1,0:T(8,128)(2,1)S(1)} %get-tuple-element.101), channel_id=1, source_target_pairs={{0,12},{2,14},{4,8},{6,10},{8,4},{10,6},{12,0},{14,2},{1,13},{3,15... | collective-permute-start | bytes 294920 | tf_op jit(solution)/shard_map/ppermute | solution.py:729
  112.4 1.4 %collective-permute-start.20 = (f16[2,192,128]{2,1,0:T(8,128)(2,1)S(1)}, f16[2,192,128]{2,1,0:T(8,128)(2,1)S(1)}, u32[]{:S(2)}, u32[]{:S(2)}) collective-permute-start(f16[2,192,128]{2,1,0:T(8,128)(2,1)S(1)} %get-tuple-element.104), channel_id=1, source_target_pairs={{0,6},{2,4},{4,2},{6,0},{8,14},{10,12},{12,10},{14,8},{1,7},{3,5},... | collective-permute-start | bytes 294920 | tf_op jit(solution)/shard_map/ppermute | solution.py:729
  114.1 4.4 %collective-permute-start.19 = (f16[2,192,128]{2,1,0:T(8,128)(2,1)S(1)}, f16[2,192,128]{2,1,0:T(8,128)(2,1)S(1)}, u32[]{:S(2)}, u32[]{:S(2)}) collective-permute-start(f16[2,192,128]{2,1,0:T(8,128)(2,1)S(1)} %get-tuple-element.105), channel_id=1, source_target_pairs={{0,4},{2,6},{4,0},{6,2},{8,12},{10,14},{12,8},{14,10},{1,5},{3,7},... | collective-permute-start | bytes 294920 | tf_op jit(solution)/shard_map/ppermute | solution.py:729
  118.5 2.4 %columns_inverse.2.refs_0_ = f32[2,128,768]{2,1,0:T(8,128)S(1)} custom-call(s32[2]{0:T(128)S(1)} %pad_add_fusion.first.token.place, f32[8,2,2,3,32,128]{5,4,3,2,1,0:T(8,128)S(1)} %convert_dynamic-update-slice_fusion.7.data, f32[4,2,128,768]{3,2,1,0:T(8,128)S(1)} %copy-done.1, f32[8,128]{1,0:T(8,128)S(1)} %get-tuple-element.53.scales, ...), custom_call_target="tpu_custom_call" | custom-call | flops 1207959552 | bytes 3145728 | tf_op jit(solution)/shard_map/columns_inverse/pallas_call | solution.py:622
  120.9 1.5 %collective-permute-done.19 = f16[2,192,128]{2,1,0:T(8,128)(2,1)S(1)} collective-permute-done((f16[2,192,128]{2,1,0:T(8,128)(2,1)S(1)}, f16[2,192,128]{2,1,0:T(8,128)(2,1)S(1)}, u32[]{:S(2)}, u32[]{:S(2)}) %collective-permute-start.19) | collective-permute-done | bytes 98336 | tf_op jit(solution)/shard_map/ppermute | solution.py:729
  122.4 0.7 collective-permute-done.18
  123.3 2.5 %columns_inverse.3 = (f32[2,128,384]{2,1,0:T(8,128)S(1)}, f32[2,128,384]{2,1,0:T(8,128)S(1)}) custom-call(s32[2]{0:T(128)S(1)} %pad_add_fusion.first.token.place, f32[8,2,2,3,32,128]{5,4,3,2,1,0:T(8,128)S(1)} %convert_dynamic-update-slice_fusion.data, f32[4,2,128,768]{3,2,1,0:T(8,128)S(1)} %copy-done.1, f32[8,128]{1,0:T(8,128)S(1)} %get-tuple-element.53.scales, ...), custom_call_target="tpu_custom_call" | custom-call | flops 1207959552 | bytes 3145728 | tf_op jit(solution)/shard_map/columns_inverse/pallas_call | solution.py:622
  125.8 1.7 %collective-permute-done.32 = f32[2,128,384]{2,1,0:T(8,128)S(1)} collective-permute-done((f32[2,128,384]{2,1,0:T(8,128)S(1)}, f32[2,128,384]{2,1,0:T(8,128)S(1)}, u32[]{:S(2)}, u32[]{:S(2)}) %collective-permute-start.32) | collective-permute-done | bytes 393248 | tf_op jit(solution)/shard_map/ppermute | solution.py:326
  127.6 0.9 multiply_add_fusion
  (99 shorter events, 1.1 us)
Async XLA Ops:
  1.1 1.5 %collective-permute-start = (f32[2,128,8]{2,1,0:T(8,128)S(1)}, f32[2,128,8]{2,1,0:T(8,128)S(1)}, u32[]{:S(2)}, u32[]{:S(2)}) collective-permute-start(f32[2,128,8]{2,1,0:T(8,128)S(1)} %slice_select_fusion), channel_id=1, source_target_pairs={{0,1},{1,0},{2,3},{3,2},{4,5},{5,4},{6,7},{7,6},{8,9},{9,8},{10,11... | collective-permute-start | bytes 24584 | tf_op jit(solution)/shard_map/ppermute | solution.py:326
  2.6 10.6 %collective-permute-start.1 = (f32[2,8,392]{2,1,0:T(8,128)S(1)}, f32[2,8,392]{2,1,0:T(8,128)S(1)}, u32[]{:S(2)}, u32[]{:S(2)}) collective-permute-start(f32[2,8,392]{2,1,0:T(8,128)S(1)} %pad_maximum_fusion), channel_id=1, source_target_pairs={{0,2},{2,4},{4,6},{6,8},{8,10},{10,12},{12,14},{1,3},{3,5},{5,7},{... | collective-permute-start | bytes 75272 | tf_op jit(solution)/shard_map/ppermute | solution.py:319
  7.4 5.9 %collective-permute-start.2 = (f32[2,8,392]{2,1,0:T(8,128)S(1)}, f32[2,8,392]{2,1,0:T(8,128)S(1)}, u32[]{:S(2)}, u32[]{:S(2)}) collective-permute-start(f32[2,8,392]{2,1,0:T(8,128)S(1)} %pad_maximum_fusion.1), channel_id=1, source_target_pairs={{2,0},{4,2},{6,4},{8,6},{10,8},{12,10},{14,12},{3,1},{5,3},{7,5},{... | collective-permute-start | bytes 75272 | tf_op jit(solution)/shard_map/ppermute | solution.py:320
  8.8 1.0 copy-start.8
  9.8 0.9 copy-start.10
  10.8 0.8 copy-start.12
  11.5 0.7 copy-start.14
  12.2 0.7 copy-start.15
  13.3 1.0 copy-start.9
  14.3 22.5 %copy-start.1 = (f32[4,2,128,768]{3,2,1,0:T(8,128)S(1)}, f32[4,2,128,768]{3,2,1,0:T(8,128)}, u32[]{:S(2)}) copy-start(f32[4,2,128,768]{3,2,1,0:T(8,128)} %maps.7) | copy-start | bytes 9437188
  14.3 22.5 %copy-start.3 = (bf16[2,512,512]{2,1,0:T(8,128)(2,1)S(1)}, bf16[2,512,512]{2,1,0:T(8,128)(2,1)}, u32[]{:S(2)}) copy-start(bf16[2,512,512]{2,1,0:T(8,128)(2,1)} %constant.36.clone.matrix) | copy-start | bytes 3145732
  14.3 22.5 %copy-start.11 = (f32[2,3,256]{2,1,0:T(4,128)S(1)}, f32[2,3,256]{2,1,0:T(4,128)}, u32[]{:S(2)}) copy-start(f32[2,3,256]{2,1,0:T(4,128)} %constant.37.clone.table) | copy-start | bytes 18436
  35.0 1.8 %collective-permute-start.3 = (f32[2,128,384]{2,1,0:T(8,128)S(1)}, f32[2,128,384]{2,1,0:T(8,128)S(1)}, u32[]{:S(2)}, u32[]{:S(2)}) collective-permute-start(f32[2,128,384]{2,1,0:T(8,128)S(1)} %get-tuple-element.52.mine), channel_id=1, source_target_pairs={{0,1},{1,0},{2,3},{3,2},{4,5},{5,4},{6,7},{7,6},{8,9},{9,8},{10,11... | collective-permute-start | bytes 1179656 | tf_op jit(solution)/shard_map/ppermute | solution.py:326
  39.3 2.6 %copy-start.5 = (f32[8,2,2,3,32,128]{5,4,3,2,1,0:T(8,128)}, f32[8,2,2,3,32,128]{5,4,3,2,1,0:T(8,128)S(1)}, u32[]{:S(2)}) copy-start(f32[8,2,2,3,32,128]{5,4,3,2,1,0:T(8,128)S(1)} %columns_forward.2) | copy-start | bytes 4718596
  41.9 1.2 copy-start.4
  41.9 12.2 %copy-start = (f32[2,96,4,1024]{3,2,1,0:T(4,128)S(1)}, f32[2,96,4,1024]{3,2,1,0:T(4,128)}, u32[]{:S(2)}) copy-start(f32[2,96,4,1024]{3,2,1,0:T(4,128)} %refs_7_.1) | copy-start | bytes 9437188
  42.0 12.1 %copy-start.2 = (s32[96,1024]{1,0:T(8,128)S(1)}, s32[96,1024]{1,0:T(8,128)}, u32[]{:S(2)}) copy-start(s32[96,1024]{1,0:T(8,128)} %refs_15_.1) | copy-start | bytes 1179652
  43.1 16.7 %collective-permute-start.16 = (f16[2,192,128]{2,1,0:T(8,128)(2,1)S(1)}, f16[2,192,128]{2,1,0:T(8,128)(2,1)S(1)}, u32[]{:S(2)}, u32[]{:S(2)}) collective-permute-start(f16[2,192,128]{2,1,0:T(8,128)(2,1)S(1)} %bitcast.164), channel_id=1, source_target_pairs={{0,12},{2,14},{4,8},{6,10},{8,4},{10,6},{12,0},{14,2},{1,13},{3,15... | collective-permute-start | bytes 294920 | tf_op jit(solution)/shard_map/ppermute | solution.py:729
  48.7 11.9 %collective-permute-start.17 = (f16[2,192,128]{2,1,0:T(8,128)(2,1)S(1)}, f16[2,192,128]{2,1,0:T(8,128)(2,1)S(1)}, u32[]{:S(2)}, u32[]{:S(2)}) collective-permute-start(f16[2,192,128]{2,1,0:T(8,128)(2,1)S(1)} %bitcast.163), channel_id=1, source_target_pairs={{0,14},{2,12},{4,10},{6,8},{8,6},{10,4},{12,2},{14,0},{1,15},{3,13... | collective-permute-start | bytes 294920 | tf_op jit(solution)/shard_map/ppermute | solution.py:729
  49.0 15.6 %collective-permute-start.15 = (f16[2,192,128]{2,1,0:T(8,128)(2,1)S(1)}, f16[2,192,128]{2,1,0:T(8,128)(2,1)S(1)}, u32[]{:S(2)}, u32[]{:S(2)}) collective-permute-start(f16[2,192,128]{2,1,0:T(8,128)(2,1)S(1)} %bitcast.162), channel_id=1, source_target_pairs={{0,10},{2,8},{4,14},{6,12},{8,2},{10,0},{12,6},{14,4},{1,11},{3,9}... | collective-permute-start | bytes 294920 | tf_op jit(solution)/shard_map/ppermute | solution.py:729
  50.7 16.4 %collective-permute-start.14 = (f16[2,192,128]{2,1,0:T(8,128)(2,1)S(1)}, f16[2,192,128]{2,1,0:T(8,128)(2,1)S(1)}, u32[]{:S(2)}, u32[]{:S(2)}) collective-permute-start(f16[2,192,128]{2,1,0:T(8,128)(2,1)S(1)} %bitcast.161), channel_id=1, source_target_pairs={{0,8},{2,10},{4,12},{6,14},{8,0},{10,2},{12,4},{14,6},{1,9},{3,11}... | collective-permute-start | bytes 294920 | tf_op jit(solution)/shard_map/ppermute | solution.py:729
  52.6 16.7 %collective-permute-start.13 = (f16[2,192,128]{2,1,0:T(8,128)(2,1)S(1)}, f16[2,192,128]{2,1,0:T(8,128)(2,1)S(1)}, u32[]{:S(2)}, u32[]{:S(2)}) collective-permute-start(f16[2,192,128]{2,1,0:T(8,128)(2,1)S(1)} %bitcast.160), channel_id=1, source_target_pairs={{0,6},{2,4},{4,2},{6,0},{8,14},{10,12},{12,10},{14,8},{1,7},{3,5},... | collective-permute-start | bytes 294920 | tf_op jit(solution)/shard_map/ppermute | solution.py:729
  54.1 19.2 %slice-start.1 = ((f32[8,2,2,3,32,128]{5,4,3,2,1,0:T(8,128)}), f32[1,2,2,3,32,128]{5,4,3,2,1,0:T(8,128)S(1)}, s32[]{:S(2)}) async-start(f32[8,2,2,3,32,128]{5,4,3,2,1,0:T(8,128)} %copy-done.5), calls=%async_computation.1 | async-start | bytes 393216 | tf_op jit(solution)/shard_map/slice | solution.py:728
  59.8 9.4 %collective-permute-start.12 = (f16[2,192,128]{2,1,0:T(8,128)(2,1)S(1)}, f16[2,192,128]{2,1,0:T(8,128)(2,1)S(1)}, u32[]{:S(2)}, u32[]{:S(2)}) collective-permute-start(f16[2,192,128]{2,1,0:T(8,128)(2,1)S(1)} %bitcast.159), channel_id=1, source_target_pairs={{0,4},{2,6},{4,0},{6,2},{8,12},{10,14},{12,8},{14,10},{1,5},{3,7},... | collective-permute-start | bytes 294920 | tf_op jit(solution)/shard_map/ppermute | solution.py:729
  60.7 12.2 %collective-permute-start.11 = (f16[2,192,128]{2,1,0:T(8,128)(2,1)S(1)}, f16[2,192,128]{2,1,0:T(8,128)(2,1)S(1)}, u32[]{:S(2)}, u32[]{:S(2)}) collective-permute-start(f16[2,192,128]{2,1,0:T(8,128)(2,1)S(1)} %bitcast.158), channel_id=1, source_target_pairs={{0,2},{2,0},{4,6},{6,4},{8,10},{10,8},{12,14},{14,12},{1,3},{3,1},... | collective-permute-start | bytes 294920 | tf_op jit(solution)/shard_map/ppermute | solution.py:729
  62.0 11.5 %copy-start.6 = (bf16[2,256,256]{2,1,0:T(8,128)(2,1)S(1)}, bf16[2,256,256]{2,1,0:T(8,128)(2,1)}, u32[]{:S(2)}) copy-start(bf16[2,256,256]{2,1,0:T(8,128)(2,1)} %constant.39.clone.inverse) | copy-start | bytes 786436
  62.0 11.5 %copy-start.7 = (bf16[2,256,256]{2,1,0:T(8,128)(2,1)S(1)}, bf16[2,256,256]{2,1,0:T(8,128)(2,1)}, u32[]{:S(2)}) copy-start(bf16[2,256,256]{2,1,0:T(8,128)(2,1)} %constant.38.clone.forward) | copy-start | bytes 786436
  62.0 11.5 %copy-start.13 = (f32[2,8,128]{2,1,0:T(8,128)S(1)}, f32[2,8,128]{2,1,0:T(8,128)}, u32[]{:S(2)}) copy-start(f32[2,8,128]{2,1,0:T(8,128)} %constant.40.clone.table) | copy-start | bytes 24580
  64.6 13.7 %collective-permute-start.9 = (f16[2,192,128]{2,1,0:T(8,128)(2,1)S(1)}, f16[2,192,128]{2,1,0:T(8,128)(2,1)S(1)}, u32[]{:S(2)}, u32[]{:S(2)}) collective-permute-start(f16[2,192,128]{2,1,0:T(8,128)(2,1)S(1)} %bitcast.157), channel_id=1, source_target_pairs={{0,12},{2,14},{4,8},{6,10},{8,4},{10,6},{12,0},{14,2},{1,13},{3,15... | collective-permute-start | bytes 294920 | tf_op jit(solution)/shard_map/ppermute | solution.py:729
  67.1 13.1 %collective-permute-start.10 = (f16[2,192,128]{2,1,0:T(8,128)(2,1)S(1)}, f16[2,192,128]{2,1,0:T(8,128)(2,1)S(1)}, u32[]{:S(2)}, u32[]{:S(2)}) collective-permute-start(f16[2,192,128]{2,1,0:T(8,128)(2,1)S(1)} %bitcast.156), channel_id=1, source_target_pairs={{0,14},{2,12},{4,10},{6,8},{8,6},{10,4},{12,2},{14,0},{1,15},{3,13... | collective-permute-start | bytes 294920 | tf_op jit(solution)/shard_map/ppermute | solution.py:729
  69.3 13.2 %collective-permute-start.8 = (f16[2,192,128]{2,1,0:T(8,128)(2,1)S(1)}, f16[2,192,128]{2,1,0:T(8,128)(2,1)S(1)}, u32[]{:S(2)}, u32[]{:S(2)}) collective-permute-start(f16[2,192,128]{2,1,0:T(8,128)(2,1)S(1)} %bitcast.155), channel_id=1, source_target_pairs={{0,10},{2,8},{4,14},{6,12},{8,2},{10,0},{12,6},{14,4},{1,11},{3,9}... | collective-permute-start | bytes 294920 | tf_op jit(solution)/shard_map/ppermute | solution.py:729
  69.3 13.4 %collective-permute-start.7 = (f16[2,192,128]{2,1,0:T(8,128)(2,1)S(1)}, f16[2,192,128]{2,1,0:T(8,128)(2,1)S(1)}, u32[]{:S(2)}, u32[]{:S(2)}) collective-permute-start(f16[2,192,128]{2,1,0:T(8,128)(2,1)S(1)} %bitcast.154), channel_id=1, source_target_pairs={{0,8},{2,10},{4,12},{6,14},{8,0},{10,2},{12,4},{14,6},{1,9},{3,11}... | collective-permute-start | bytes 294920 | tf_op jit(solution)/shard_map/ppermute | solution.py:729
  72.8 9.9 %collective-permute-start.6 = (f16[2,192,128]{2,1,0:T(8,128)(2,1)S(1)}, f16[2,192,128]{2,1,0:T(8,128)(2,1)S(1)}, u32[]{:S(2)}, u32[]{:S(2)}) collective-permute-start(f16[2,192,128]{2,1,0:T(8,128)(2,1)S(1)} %bitcast.153), channel_id=1, source_target_pairs={{0,6},{2,4},{4,2},{6,0},{8,14},{10,12},{12,10},{14,8},{1,7},{3,5},... | collective-permute-start | bytes 294920 | tf_op jit(solution)/shard_map/ppermute | solution.py:729
  77.9 14.7 %slice-start = ((f32[8,2,2,3,32,128]{5,4,3,2,1,0:T(8,128)}), f32[1,2,2,3,32,128]{5,4,3,2,1,0:T(8,128)S(1)}, s32[]{:S(2)}) async-start(f32[8,2,2,3,32,128]{5,4,3,2,1,0:T(8,128)} %copy-done.4), calls=%async_computation | async-start | bytes 393216 | tf_op jit(solution)/shard_map/slice | solution.py:728
  78.3 5.8 %collective-permute-start.5 = (f16[2,192,128]{2,1,0:T(8,128)(2,1)S(1)}, f16[2,192,128]{2,1,0:T(8,128)(2,1)S(1)}, u32[]{:S(2)}, u32[]{:S(2)}) collective-permute-start(f16[2,192,128]{2,1,0:T(8,128)(2,1)S(1)} %bitcast.152), channel_id=1, source_target_pairs={{0,4},{2,6},{4,0},{6,2},{8,12},{10,14},{12,8},{14,10},{1,5},{3,7},... | collective-permute-start | bytes 294920 | tf_op jit(solution)/shard_map/ppermute | solution.py:729
  80.2 4.6 %collective-permute-start.4 = (f16[2,192,128]{2,1,0:T(8,128)(2,1)S(1)}, f16[2,192,128]{2,1,0:T(8,128)(2,1)S(1)}, u32[]{:S(2)}, u32[]{:S(2)}) collective-permute-start(f16[2,192,128]{2,1,0:T(8,128)(2,1)S(1)} %bitcast.151), channel_id=1, source_target_pairs={{0,2},{2,0},{4,6},{6,4},{8,10},{10,8},{12,14},{14,12},{1,3},{3,1},... | collective-permute-start | bytes 294920 | tf_op jit(solution)/shard_map/ppermute | solution.py:729
  84.8 13.0 %collective-permute-start.31 = (f16[2,192,128]{2,1,0:T(8,128)(2,1)S(1)}, f16[2,192,128]{2,1,0:T(8,128)(2,1)S(1)}, u32[]{:S(2)}, u32[]{:S(2)}) collective-permute-start(f16[2,192,128]{2,1,0:T(8,128)(2,1)S(1)} %get-tuple-element.93), channel_id=1, source_target_pairs={{0,14},{2,12},{4,10},{6,8},{8,6},{10,4},{12,2},{14,0},{1,15},{3,13... | collective-permute-start | bytes 294920 | tf_op jit(solution)/shard_map/ppermute | solution.py:729
  87.4 12.9 %collective-permute-start.30 = (f16[2,192,128]{2,1,0:T(8,128)(2,1)S(1)}, f16[2,192,128]{2,1,0:T(8,128)(2,1)S(1)}, u32[]{:S(2)}, u32[]{:S(2)}) collective-permute-start(f16[2,192,128]{2,1,0:T(8,128)(2,1)S(1)} %get-tuple-element.94), channel_id=1, source_target_pairs={{0,12},{2,14},{4,8},{6,10},{8,4},{10,6},{12,0},{14,2},{1,13},{3,15... | collective-permute-start | bytes 294920 | tf_op jit(solution)/shard_map/ppermute | solution.py:729
  89.2 13.7 %collective-permute-start.29 = (f16[2,192,128]{2,1,0:T(8,128)(2,1)S(1)}, f16[2,192,128]{2,1,0:T(8,128)(2,1)S(1)}, u32[]{:S(2)}, u32[]{:S(2)}) collective-permute-start(f16[2,192,128]{2,1,0:T(8,128)(2,1)S(1)} %get-tuple-element.95), channel_id=1, source_target_pairs={{0,10},{2,8},{4,14},{6,12},{8,2},{10,0},{12,6},{14,4},{1,11},{3,9}... | collective-permute-start | bytes 294920 | tf_op jit(solution)/shard_map/ppermute | solution.py:729
  89.2 17.5 %collective-permute-start.28 = (f16[2,192,128]{2,1,0:T(8,128)(2,1)S(1)}, f16[2,192,128]{2,1,0:T(8,128)(2,1)S(1)}, u32[]{:S(2)}, u32[]{:S(2)}) collective-permute-start(f16[2,192,128]{2,1,0:T(8,128)(2,1)S(1)} %get-tuple-element.96), channel_id=1, source_target_pairs={{0,8},{2,10},{4,12},{6,14},{8,0},{10,2},{12,4},{14,6},{1,9},{3,11}... | collective-permute-start | bytes 294920 | tf_op jit(solution)/shard_map/ppermute | solution.py:729
  92.5 19.9 %collective-permute-start.27 = (f16[2,192,128]{2,1,0:T(8,128)(2,1)S(1)}, f16[2,192,128]{2,1,0:T(8,128)(2,1)S(1)}, u32[]{:S(2)}, u32[]{:S(2)}) collective-permute-start(f16[2,192,128]{2,1,0:T(8,128)(2,1)S(1)} %get-tuple-element.97), channel_id=1, source_target_pairs={{0,6},{2,4},{4,2},{6,0},{8,14},{10,12},{12,10},{14,8},{1,7},{3,5},... | collective-permute-start | bytes 294920 | tf_op jit(solution)/shard_map/ppermute | solution.py:729
  97.8 14.6 %collective-permute-start.26 = (f16[2,192,128]{2,1,0:T(8,128)(2,1)S(1)}, f16[2,192,128]{2,1,0:T(8,128)(2,1)S(1)}, u32[]{:S(2)}, u32[]{:S(2)}) collective-permute-start(f16[2,192,128]{2,1,0:T(8,128)(2,1)S(1)} %get-tuple-element.98), channel_id=1, source_target_pairs={{0,4},{2,6},{4,0},{6,2},{8,12},{10,14},{12,8},{14,10},{1,5},{3,7},... | collective-permute-start | bytes 294920 | tf_op jit(solution)/shard_map/ppermute | solution.py:729
  100.3 12.1 %collective-permute-start.25 = (f16[2,192,128]{2,1,0:T(8,128)(2,1)S(1)}, f16[2,192,128]{2,1,0:T(8,128)(2,1)S(1)}, u32[]{:S(2)}, u32[]{:S(2)}) collective-permute-start(f16[2,192,128]{2,1,0:T(8,128)(2,1)S(1)} %get-tuple-element.99), channel_id=1, source_target_pairs={{0,2},{2,0},{4,6},{6,4},{8,10},{10,8},{12,14},{14,12},{1,3},{3,1},... | collective-permute-start | bytes 294920 | tf_op jit(solution)/shard_map/ppermute | solution.py:729
  103.0 11.1 %collective-permute-start.24 = (f16[2,192,128]{2,1,0:T(8,128)(2,1)S(1)}, f16[2,192,128]{2,1,0:T(8,128)(2,1)S(1)}, u32[]{:S(2)}, u32[]{:S(2)}) collective-permute-start(f16[2,192,128]{2,1,0:T(8,128)(2,1)S(1)} %get-tuple-element.100), channel_id=1, source_target_pairs={{0,14},{2,12},{4,10},{6,8},{8,6},{10,4},{12,2},{14,0},{1,15},{3,13... | collective-permute-start | bytes 294920 | tf_op jit(solution)/shard_map/ppermute | solution.py:729
  106.8 11.7 %collective-permute-start.23 = (f16[2,192,128]{2,1,0:T(8,128)(2,1)S(1)}, f16[2,192,128]{2,1,0:T(8,128)(2,1)S(1)}, u32[]{:S(2)}, u32[]{:S(2)}) collective-permute-start(f16[2,192,128]{2,1,0:T(8,128)(2,1)S(1)} %get-tuple-element.101), channel_id=1, source_target_pairs={{0,12},{2,14},{4,8},{6,10},{8,4},{10,6},{12,0},{14,2},{1,13},{3,15... | collective-permute-start | bytes 294920 | tf_op jit(solution)/shard_map/ppermute | solution.py:729
  112.3 8.5 %collective-permute-start.22 = (f16[2,192,128]{2,1,0:T(8,128)(2,1)S(1)}, f16[2,192,128]{2,1,0:T(8,128)(2,1)S(1)}, u32[]{:S(2)}, u32[]{:S(2)}) collective-permute-start(f16[2,192,128]{2,1,0:T(8,128)(2,1)S(1)} %get-tuple-element.102), channel_id=1, source_target_pairs={{0,10},{2,8},{4,14},{6,12},{8,2},{10,0},{12,6},{14,4},{1,11},{3,9}... | collective-permute-start | bytes 294920 | tf_op jit(solution)/shard_map/ppermute | solution.py:729
  112.3 8.5 %collective-permute-start.21 = (f16[2,192,128]{2,1,0:T(8,128)(2,1)S(1)}, f16[2,192,128]{2,1,0:T(8,128)(2,1)S(1)}, u32[]{:S(2)}, u32[]{:S(2)}) collective-permute-start(f16[2,192,128]{2,1,0:T(8,128)(2,1)S(1)} %get-tuple-element.103), channel_id=1, source_target_pairs={{0,8},{2,10},{4,12},{6,14},{8,0},{10,2},{12,4},{14,6},{1,9},{3,11}... | collective-permute-start | bytes 294920 | tf_op jit(solution)/shard_map/ppermute | solution.py:729
  112.4 8.5 %collective-permute-start.20 = (f16[2,192,128]{2,1,0:T(8,128)(2,1)S(1)}, f16[2,192,128]{2,1,0:T(8,128)(2,1)S(1)}, u32[]{:S(2)}, u32[]{:S(2)}) collective-permute-start(f16[2,192,128]{2,1,0:T(8,128)(2,1)S(1)} %get-tuple-element.104), channel_id=1, source_target_pairs={{0,6},{2,4},{4,2},{6,0},{8,14},{10,12},{12,10},{14,8},{1,7},{3,5},... | collective-permute-start | bytes 294920 | tf_op jit(solution)/shard_map/ppermute | solution.py:729
  114.1 8.3 %collective-permute-start.19 = (f16[2,192,128]{2,1,0:T(8,128)(2,1)S(1)}, f16[2,192,128]{2,1,0:T(8,128)(2,1)S(1)}, u32[]{:S(2)}, u32[]{:S(2)}) collective-permute-start(f16[2,192,128]{2,1,0:T(8,128)(2,1)S(1)} %get-tuple-element.105), channel_id=1, source_target_pairs={{0,4},{2,6},{4,0},{6,2},{8,12},{10,14},{12,8},{14,10},{1,5},{3,7},... | collective-permute-start | bytes 294920 | tf_op jit(solution)/shard_map/ppermute | solution.py:729
  118.5 4.6 %collective-permute-start.18 = (f16[2,192,128]{2,1,0:T(8,128)(2,1)S(1)}, f16[2,192,128]{2,1,0:T(8,128)(2,1)S(1)}, u32[]{:S(2)}, u32[]{:S(2)}) collective-permute-start(f16[2,192,128]{2,1,0:T(8,128)(2,1)S(1)} %get-tuple-element.106), channel_id=1, source_target_pairs={{0,2},{2,0},{4,6},{6,4},{8,10},{10,8},{12,14},{14,12},{1,3},{3,1},... | collective-permute-start | bytes 294920 | tf_op jit(solution)/shard_map/ppermute | solution.py:729
  123.3 4.3 %copy-start.16 = (f32[2,128,384]{2,1,0:T(8,128)S(1)}, f32[2,128,384]{2,1,0:T(8,128)}, u32[]{:S(2)}) copy-start(f32[2,128,384]{2,1,0:T(8,128)} %param.25) | copy-start | bytes 1179652
  125.8 1.8 %collective-permute-start.32 = (f32[2,128,384]{2,1,0:T(8,128)S(1)}, f32[2,128,384]{2,1,0:T(8,128)S(1)}, u32[]{:S(2)}, u32[]{:S(2)}) collective-permute-start(f32[2,128,384]{2,1,0:T(8,128)S(1)} %get-tuple-element.91), channel_id=1, source_target_pairs={{0,1},{1,0},{2,3},{3,2},{4,5},{5,4},{6,7},{7,6},{8,9},{9,8},{10,11... | collective-permute-start | bytes 1179656 | tf_op jit(solution)/shard_map/ppermute | solution.py:326
where the time goes:
time: 129 us; the launch traced here: 128 us
  starting transfers between devices  58.4 us (45%)
  Pallas kernels  45.6 us (35%)
  waiting for transfers between devices  13.1 us (10%)
  local copies, waits for them, and re-layouts  7.37 us (6%)
  other arithmetic  3.3 us (3%)
    ppermute x28, starting transfers between devices, send(): lax.ppermute(value[k].astype(jnp.float16), 'gz', [(i, i ^ k) for i in ran...  51.7 us
    pallas_call x1, Pallas kernels, run_network(): pl.pallas_call(network_kernel, out_shape=(shape, shape), in_specs=[pl.Blo...  20.7 us
    ppermute x28, waiting for transfers between devices, send(): lax.ppermute(value[k].astype(jnp.float16), 'gz', [(i, i ^ k) for i in ran...  9.57 us
    pallas_call x2, Pallas kernels, rows_both_ways(): pl.pallas_call(rows_kernel, out_shape=jax.ShapeDtypeStruct(data.shape, F3...  8.99 us
    unnamed x38, local copies, waits for them, and re-layouts  5.98 us
    pallas_call x1, Pallas kernels, prepare_target(): pl.pallas_call(partial(target_kernel, radix3), out_shape=(jax.ShapeDtypeS...  5.72 us
    pallas_call x2, Pallas kernels, columns_inverse(): pl.pallas_call(partial(columns_inverse_kernel, last), out_shape=shape, gr...  4.9 us
    pallas_call x2, Pallas kernels, columns_forward(): pl.pallas_call(columns_forward_kernel, out_shape=jax.ShapeDtypeStruct((gr...  4.86 us
  transfers between devices with their start and end apart: 33, of which 11 were waited for; matrix products, arithmetic and copies ran while one was open for 2% of the time, Pallas kernels for 14%

commit v1 on v0

--- a/solution.py
+++ b/solution.py
@@ -64,19 +64,19 @@
     return np.stack(first), middle, np.stack(last)
 
 
-def weights_kernel(cols, height, first_taps, k2, last_taps, choice1, choice3, first, inner, last, scales):
+def weights_kernel(cols, height, first_taps, k2, last_taps, choice, first, inner, last, scales):
     _, middle, _ = tap_choices()
     ch = k2.shape[1]
     k1 = jnp.concatenate([first_taps[t].astype(F32) for t in range(9)], axis=0).astype(BF16)
     k3 = jnp.concatenate([last_taps[t].astype(F32) for t in range(9)], axis=0).astype(BF16)
-    parts = [mm(choice1[i], k1) for i in range(4)]
+    parts = [mm(choice[i, 0:512], k1) for i in range(4)]
     first[...] = (0.5 * jnp.concatenate(parts, axis=1)).astype(BF16).reshape(first.shape)
     turned = [(0.5 * jnp.transpose(k2[t].astype(F32))).astype(BF16) for t in range(9)]
     zero = jnp.zeros((ch, ch), BF16)
     for p, taps in enumerate(middle):
         row = [zero if t is None else turned[t] for t in taps]
         inner[p * ch : (p + 1) * ch, :] = jnp.concatenate(row, axis=1)
-    parts = [mm(choice3[i], k3) for i in range(4)]
+    parts = [mm(choice[i, 512:544], k3) for i in range(4)]
     last[...] = jnp.concatenate(parts, axis=1).astype(BF16)
 
     def top(value, axes):
@@ -118,8 +118,7 @@
         jnp.transpose(first_kernel, (0, 2, 1)),
         inner_kernel,
         last_kernel,
-        jnp.asarray(choice1, BF16),
-        jnp.asarray(choice3, BF16),
+        jnp.asarray(np.concatenate([choice1, choice3], axis=1), BF16),
     )
     return (first, inner, last), scales
 
@@ -142,7 +141,6 @@
 ):
     rows, cols = center.shape[1:]
     blocks = rows // 2 + 2
-    groups = q.shape[1] // 8 - 1
     used = hid.shape[1]
     step = done.shape[0] // used
 
@@ -168,7 +166,8 @@
         both = mm(tile[...].reshape(-1, cols).astype(BF16), sel)
         both += mm(edge, sel_side)
         for ch in range(2):
-            q[4 * ch + d] = both[ch * (rows + 16) : (ch + 1) * (rows + 16)]
+            q[4 * ch + d, 0 : rows + 16] = both[ch * (rows + 16) : (ch + 1) * (rows + 16)]
+            q[4 * ch + d, rows + 16 :] = jnp.zeros((8, 256), F32)
 
     end = cols // 2 + 1
     tail = end // 8 * 8
@@ -193,18 +192,21 @@
     hid[0] = jnp.zeros(hid.shape[1:], BF16)
     hid_side[0] = jnp.zeros(hid.shape[1:], BF16)
 
-    def first_layer(t, carry):
-        window = q[:, pl.ds(pl.multiple_of(8 * t, 8), 16), :].reshape(128, 256)
-        window = jnp.transpose(window)[:used].astype(BF16)
-        for s in range(4):
-            h = silu_rows(mm(window, first[s]))
-            place = 4 * t + s + 1
-            hid[place] = h.astype(BF16)
-            hid_side[place, :, 0:128] = pltpu.roll(h[:, 128:256], 1, 0).astype(BF16)
-            hid_side[place, :, 128:256] = pltpu.roll(h[:, 0:128], used - 1, 0).astype(BF16)
+    def first_layer(pair, carry):
+        windows = []
+        for t in (2 * pair, 2 * pair + 1):
+            window = q[:, pl.ds(pl.multiple_of(8 * t, 8), 16), :].reshape(128, 256)
+            windows.append(jnp.transpose(window)[:used].astype(BF16))
+        for n, window in enumerate(windows):
+            for s in range(4):
+                h = silu_rows(mm(window, first[s]))
+                place = 8 * pair + 4 * n + s + 1
+                hid[place] = h.astype(BF16)
+                hid_side[place, :, 0:128] = pltpu.roll(h[:, 128:256], 1, 0).astype(BF16)
+                hid_side[place, :, 128:256] = pltpu.roll(h[:, 0:128], used - 1, 0).astype(BF16)
         return carry
 
-    lax.fori_loop(0, groups, first_layer, 0)
+    lax.fori_loop(0, (hid.shape[0] - 1) // 8, first_layer, 0)
 
     for flag, j in ((0, 0), (1, blocks - 1)):
 
@@ -282,7 +284,7 @@
 def run_network(noisy, top, bottom, side, flags, weights):
     _, rows, cols = noisy.shape
     blocks = rows // 2 + 2
-    groups = -(-blocks // 4)
+    pairs = -(-blocks // 8)
     used = ceil_to(cols // 2 + 2, 16)
     step = max(u for u in (1, 2, 3, 6) if blocks % u == 0)
     vmem = pl.BlockSpec(memory_space=pltpu.VMEM)
@@ -294,9 +296,9 @@
         out_specs=(vmem, vmem),
         scratch_shapes=[
             pltpu.VMEM((2, rows + 16, cols), F32),
-            pltpu.VMEM((8, 8 * groups + 8, 256), F32),
-            pltpu.VMEM((4 * groups + 1, used, 256), BF16),
-            pltpu.VMEM((4 * groups + 1, used, 256), BF16),
+            pltpu.VMEM((8, rows + 24, 256), F32),
+            pltpu.VMEM((8 * pairs + 1, used, 256), BF16),
+            pltpu.VMEM((8 * pairs + 1, used, 256), BF16),
             pltpu.VMEM((step * used, 256), BF16),
             pltpu.VMEM((2, 16 * (blocks + step) + 16, 128), F32),
         ],
@@ -526,7 +528,7 @@
     forward = halves(np.block([[c, -s], [s, c]]))
     inverse = halves(np.block([[c, s], [-s, c]]))
     table = turn_table(radix, LANES)
-    block = max(b for b in range(8, 56, 8) if pencil % b == 0)
+    block = max(b for b in range(8, 104, 8) if pencil % b == 0)
     offset, repeat = first_line // block, pencil // block
     vmem = pl.BlockSpec(memory_space=pltpu.VMEM)
     spec = pl.BlockSpec((radix, 2, block, LANES), lambda i: (0, 0, i, 0))
@@ -677,11 +679,12 @@
                 lines[start : start + per, t * LANES : (t + 1) * LANES] = source[
                     pl.ds(q * coils + c, per, stride=radix3 * coils), :
                 ]
-    high, low = split2(lines[...])
+    both = jnp.concatenate(split2(lines[...]), axis=0)
     for q in range(0, radix, 2):
         width = min(2, radix - q) * LANES
         part = order[:, q * LANES : q * LANES + width]
-        picked = mm(high, part) + mm(low, part)
+        picked = mm(both, part)
+        picked = picked[:count] + picked[count:]
         for k in range(0, width, LANES):
             target[0, q + k // LANES] = picked[:, k : k + LANES]
 

time: 129 us -> 125 us (0.969)
  starting transfers between devices: 58.4 us -> 51.9 us
  waiting for transfers between devices: 13.1 us -> 19.5 us
  Pallas kernels: 45.6 us -> 42.8 us
    ppermute x28, starting transfers between devices: 51.7 us -> 45.1 us  [send(): lax.ppermute(value[k].astype(jnp.float16), 'gz', [(i, i ^ k) for i in ran...]
    ppermute x28, waiting for transfers between devices: 9.57 us -> 15.3 us  [send(): lax.ppermute(value[k].astype(jnp.float16), 'gz', [(i, i ^ k) for i in ran...]
    pallas_call x1, Pallas kernels: 20.7 us -> 19.3 us  [run_network(): pl.pallas_call(network_kernel, out_shape=(shape, shape), in_specs=[pl.Blo...]
    pallas_call x2, Pallas kernels: 8.99 us -> 7.65 us  [rows_both_ways(): pl.pallas_call(rows_kernel, out_shape=jax.ShapeDtypeStruct(data.shape, F3...]
    unnamed x38 -> x36, local copies, waits for them, and re-layouts: 5.98 us -> 5.24 us
  transfers between devices with their start and end apart: 33 -> 33, of which waited for: 11 -> 15; matrix products, arithmetic and copies ran while one was open for 2% -> 2% of each run, Pallas kernels for 14% -> 13%
where the time goes in v1:
time: 125 us
  starting transfers between devices  51.9 us (42%)
  Pallas kernels  42.8 us (34%)
  waiting for transfers between devices  19.5 us (16%)
  local copies, waits for them, and re-layouts  6.64 us (5%)
  other arithmetic  3.3 us (3%)
    ppermute x28, starting transfers between devices, send(): lax.ppermute(value[k].astype(jnp.float16), 'gz', [(i, i ^ k) for i in ran...  45.1 us
    pallas_call x1, Pallas kernels, run_network(): pl.pallas_call(network_kernel, out_shape=(shape, shape), in_specs=[pl.Blo...  19.3 us
    ppermute x28, waiting for transfers between devices, send(): lax.ppermute(value[k].astype(jnp.float16), 'gz', [(i, i ^ k) for i in ran...  15.3 us
    pallas_call x2, Pallas kernels, rows_both_ways(): pl.pallas_call(rows_kernel, out_shape=jax.ShapeDtypeStruct(data.shape, F3...  7.65 us
    pallas_call x1, Pallas kernels, prepare_target(): pl.pallas_call(partial(target_kernel, radix3), out_shape=(jax.ShapeDtypeS...  5.68 us
    unnamed x36, local copies, waits for them, and re-layouts  5.24 us
    pallas_call x2, Pallas kernels, columns_inverse(): pl.pallas_call(partial(columns_inverse_kernel, last), out_shape=shape, gr...  4.89 us
    pallas_call x2, Pallas kernels, columns_forward(): pl.pallas_call(columns_forward_kernel, out_shape=jax.ShapeDtypeStruct((gr...  4.86 us
  transfers between devices with their start and end apart: 33, of which 15 were waited for; matrix products, arithmetic and copies ran while one was open for 2% of the time, Pallas kernels for 13%

profile of v1, /device:TPU:0, one launch (start us, length us, event | category | flops | bytes accessed | tf_op | source)
XLA Modules:
  0.0 124.8 jit_solution(9269173385815324683)
XLA Ops:
  0.0 1.1 slice_select_fusion
  1.1 0.6 collective-permute-start
  1.6 0.8 fusion.2
  2.4 0.2 collective-permute-done.side
  2.6 4.8 %collective-permute-start.1 = (f32[2,8,392]{2,1,0:T(8,128)S(1)}, f32[2,8,392]{2,1,0:T(8,128)S(1)}, u32[]{:S(2)}, u32[]{:S(2)}) collective-permute-start(f32[2,8,392]{2,1,0:T(8,128)S(1)} %pad_maximum_fusion), channel_id=1, source_target_pairs={{0,2},{2,4},{4,6},{6,8},{8,10},{10,12},{12,14},{1,3},{3,5},{5,7},{... | collective-permute-start | bytes 75272 | tf_op jit(solution)/shard_map/ppermute | solution.py:321
  7.4 1.3 %collective-permute-start.2 = (f32[2,8,392]{2,1,0:T(8,128)S(1)}, f32[2,8,392]{2,1,0:T(8,128)S(1)}, u32[]{:S(2)}, u32[]{:S(2)}) collective-permute-start(f32[2,8,392]{2,1,0:T(8,128)S(1)} %pad_maximum_fusion.1), channel_id=1, source_target_pairs={{2,0},{4,2},{6,4},{8,6},{10,8},{12,10},{14,12},{3,1},{5,3},{7,5},{... | collective-permute-start | bytes 75272 | tf_op jit(solution)/shard_map/ppermute | solution.py:322
  8.8 1.1 copy-done.8
  9.9 0.9 copy-done.10
  10.8 0.7 copy-done.13
  11.5 0.7 copy-done.14
  12.1 0.4 weights.1
  12.5 0.7 collective-permute-done.2.bottom
  13.2 1.0 copy-done.9
  14.2 19.3 %network.1 = (f32[2,128,384]{2,1,0:T(8,128)S(1)}, f32[2,128,384]{2,1,0:T(8,128)S(1)}) custom-call(s32[4]{0:T(128)S(1)} %add_convert_fusion.flags, f32[2,8,392]{2,1,0:T(8,128)S(1)} %collective-permute-done.1.top, f32[2,128,384]{2,1,0:T(8,128)S(1)} %copy-done.9, f32[2,8,392]{2,1,0:T(8,128)S(1)} %collective-permute-done.2.bottom, ...), custom_call_target="tpu_custom_call" | custom-call | flops 4026531840 | bytes 1179648 | tf_op jit(solution)/shard_map/network/pallas_call | solution.py:292
  33.7 1.6 %collective-permute-done.3.other = f32[2,128,384]{2,1,0:T(8,128)S(1)} collective-permute-done((f32[2,128,384]{2,1,0:T(8,128)S(1)}, f32[2,128,384]{2,1,0:T(8,128)S(1)}, u32[]{:S(2)}, u32[]{:S(2)}) %collective-permute-start.3) | collective-permute-done | bytes 393248 | tf_op jit(solution)/shard_map/ppermute | solution.py:328
  35.4 2.4 %columns_forward.2 = f32[8,2,2,3,32,128]{5,4,3,2,1,0:T(8,128)S(1)} custom-call(s32[2]{0:T(128)S(1)} %pad_add_fusion.first.token.place, f32[2,128,384]{2,1,0:T(8,128)S(1)} %get-tuple-element.52.mine, f32[2,128,384]{2,1,0:T(8,128)S(1)} %collective-permute-done.3.other, f32[4,2,128,768]{3,2,1,0:T(8,128)S(1)} %copy-done.1, ...), custom_call_target="tpu_custom_call" | custom-call | flops 1207959552 | bytes 3145728 | tf_op jit(solution)/shard_map/columns_forward/pallas_call | solution.py:463
  37.8 0.2 convert.66
  38.0 2.4 %columns_forward.3 = f32[8,2,2,3,32,128]{5,4,3,2,1,0:T(8,128)S(1)} custom-call(s32[2]{0:T(128)S(1)} %pad_add_fusion.first.token.place, f32[2,128,384]{2,1,0:T(8,128)S(1)} %get-tuple-element.52.mine, f32[2,128,384]{2,1,0:T(8,128)S(1)} %collective-permute-done.3.other, f32[4,2,128,768]{3,2,1,0:T(8,128)S(1)} %copy-done.1, ...), custom_call_target="tpu_custom_call" | custom-call | flops 1207959552 | bytes 3145728 | tf_op jit(solution)/shard_map/columns_forward/pallas_call | solution.py:463
  40.5 0.2 convert.65
  40.9 0.8 copy-done.4
  41.7 4.9 %collective-permute-start.16 = (f16[2,192,128]{2,1,0:T(8,128)(2,1)S(1)}, f16[2,192,128]{2,1,0:T(8,128)(2,1)S(1)}, u32[]{:S(2)}, u32[]{:S(2)}) collective-permute-start(f16[2,192,128]{2,1,0:T(8,128)(2,1)S(1)} %bitcast.164), channel_id=1, source_target_pairs={{0,12},{2,14},{4,8},{6,10},{8,4},{10,6},{12,0},{14,2},{1,13},{3,15... | collective-permute-start | bytes 294920 | tf_op jit(solution)/shard_map/ppermute | solution.py:732
  46.6 0.7 collective-permute-start.17
  47.3 1.2 collective-permute-start.15
  48.5 1.9 %collective-permute-start.14 = (f16[2,192,128]{2,1,0:T(8,128)(2,1)S(1)}, f16[2,192,128]{2,1,0:T(8,128)(2,1)S(1)}, u32[]{:S(2)}, u32[]{:S(2)}) collective-permute-start(f16[2,192,128]{2,1,0:T(8,128)(2,1)S(1)} %bitcast.161), channel_id=1, source_target_pairs={{0,8},{2,10},{4,12},{6,14},{8,0},{10,2},{12,4},{14,6},{1,9},{3,11}... | collective-permute-start | bytes 294920 | tf_op jit(solution)/shard_map/ppermute | solution.py:732
  50.4 1.5 %collective-permute-start.13 = (f16[2,192,128]{2,1,0:T(8,128)(2,1)S(1)}, f16[2,192,128]{2,1,0:T(8,128)(2,1)S(1)}, u32[]{:S(2)}, u32[]{:S(2)}) collective-permute-start(f16[2,192,128]{2,1,0:T(8,128)(2,1)S(1)} %bitcast.160), channel_id=1, source_target_pairs={{0,6},{2,4},{4,2},{6,0},{8,14},{10,12},{12,10},{14,8},{1,7},{3,5},... | collective-permute-start | bytes 294920 | tf_op jit(solution)/shard_map/ppermute | solution.py:732
  52.0 5.7 %target.1 = (f32[2,8,384,128]{3,2,1,0:T(8,128)S(1)}, f32[8,96,128]{2,1,0:T(8,128)S(1)}) custom-call(s32[2]{0:T(128)S(1)} %pad_add_fusion.first.token.place, f32[2,96,4,1024]{3,2,1,0:T(4,128)S(1)} %copy-done, f32[2,96,4,1024]{3,2,1,0:T(4,128)S(1)} %copy-done, f32[2,96,4,1024]{3,2,1,0:T(4,128)S(1)} %copy-done, f32[2,96,4,1024]{3,2,1,0:T(4,128)S(1)} %copy-done, ...), custom_call_target="tpu_custom_call" | custom-call | flops 3221225472 | bytes 6291456 | tf_op jit(solution)/shard_map/target/pallas_call | solution.py:696
  57.7 1.3 %collective-permute-start.12 = (f16[2,192,128]{2,1,0:T(8,128)(2,1)S(1)}, f16[2,192,128]{2,1,0:T(8,128)(2,1)S(1)}, u32[]{:S(2)}, u32[]{:S(2)}) collective-permute-start(f16[2,192,128]{2,1,0:T(8,128)(2,1)S(1)} %bitcast.159), channel_id=1, source_target_pairs={{0,4},{2,6},{4,0},{6,2},{8,12},{10,14},{12,8},{14,10},{1,5},{3,7},... | collective-permute-start | bytes 294920 | tf_op jit(solution)/shard_map/ppermute | solution.py:732
  59.0 0.7 collective-permute-start.11
  59.9 3.1 %collective-permute-done.15 = f16[2,192,128]{2,1,0:T(8,128)(2,1)S(1)} collective-permute-done((f16[2,192,128]{2,1,0:T(8,128)(2,1)S(1)}, f16[2,192,128]{2,1,0:T(8,128)(2,1)S(1)}, u32[]{:S(2)}, u32[]{:S(2)}) %collective-permute-start.15) | collective-permute-done | bytes 98336 | tf_op jit(solution)/shard_map/ppermute | solution.py:732
  62.9 2.5 %collective-permute-start.9 = (f16[2,192,128]{2,1,0:T(8,128)(2,1)S(1)}, f16[2,192,128]{2,1,0:T(8,128)(2,1)S(1)}, u32[]{:S(2)}, u32[]{:S(2)}) collective-permute-start(f16[2,192,128]{2,1,0:T(8,128)(2,1)S(1)} %bitcast.157), channel_id=1, source_target_pairs={{0,12},{2,14},{4,8},{6,10},{8,4},{10,6},{12,0},{14,2},{1,13},{3,15... | collective-permute-start | bytes 294920 | tf_op jit(solution)/shard_map/ppermute | solution.py:732
  65.4 1.8 %collective-permute-start.10 = (f16[2,192,128]{2,1,0:T(8,128)(2,1)S(1)}, f16[2,192,128]{2,1,0:T(8,128)(2,1)S(1)}, u32[]{:S(2)}, u32[]{:S(2)}) collective-permute-start(f16[2,192,128]{2,1,0:T(8,128)(2,1)S(1)} %bitcast.156), channel_id=1, source_target_pairs={{0,14},{2,12},{4,10},{6,8},{8,6},{10,4},{12,2},{14,0},{1,15},{3,13... | collective-permute-start | bytes 294920 | tf_op jit(solution)/shard_map/ppermute | solution.py:732
  67.2 3.5 %collective-permute-start.7 = (f16[2,192,128]{2,1,0:T(8,128)(2,1)S(1)}, f16[2,192,128]{2,1,0:T(8,128)(2,1)S(1)}, u32[]{:S(2)}, u32[]{:S(2)}) collective-permute-start(f16[2,192,128]{2,1,0:T(8,128)(2,1)S(1)} %bitcast.154), channel_id=1, source_target_pairs={{0,8},{2,10},{4,12},{6,14},{8,0},{10,2},{12,4},{14,6},{1,9},{3,11}... | collective-permute-start | bytes 294920 | tf_op jit(solution)/shard_map/ppermute | solution.py:732
  70.7 0.5 collective-permute-start.6
  71.4 3.7 %rows_both_ways.2 = f32[8,2,192,128]{3,2,1,0:T(8,128)S(1)} custom-call(s32[2]{0:T(128)S(1)} %pad_add_fusion.first.token.place, f32[8,2,192,128]{3,2,1,0:T(8,128)S(1)} %convert_dynamic-update-slice_fusion.21.data, f32[8,96,128]{2,1,0:T(8,128)S(1)} %get-tuple-element.64.kept, f32[2,8,384,128]{3,2,1,0:T(8,128)S(1)} %get-tuple-element.65.target, ...), custom_call_target="tpu_custom_call" | custom-call | flops 603979776 | bytes 6291456 | tf_op jit(solution)/shard_map/rows_both_ways/pallas_call | solution.py:535
  75.3 0.2 slice_bitcast_fusion.2
  75.5 2.0 %collective-permute-start.5 = (f16[2,192,128]{2,1,0:T(8,128)(2,1)S(1)}, f16[2,192,128]{2,1,0:T(8,128)(2,1)S(1)}, u32[]{:S(2)}, u32[]{:S(2)}) collective-permute-start(f16[2,192,128]{2,1,0:T(8,128)(2,1)S(1)} %bitcast.152), channel_id=1, source_target_pairs={{0,4},{2,6},{4,0},{6,2},{8,12},{10,14},{12,8},{14,10},{1,5},{3,7},... | collective-permute-start | bytes 294920 | tf_op jit(solution)/shard_map/ppermute | solution.py:732
  77.4 1.1 collective-permute-start.4
  78.5 1.6 %collective-permute-done.8 = f16[2,192,128]{2,1,0:T(8,128)(2,1)S(1)} collective-permute-done((f16[2,192,128]{2,1,0:T(8,128)(2,1)S(1)}, f16[2,192,128]{2,1,0:T(8,128)(2,1)S(1)}, u32[]{:S(2)}, u32[]{:S(2)}) %collective-permute-start.8) | collective-permute-done | bytes 98336 | tf_op jit(solution)/shard_map/ppermute | solution.py:732
  80.2 0.9 collective-permute-done.7
  81.0 1.0 collective-permute-done.5
  82.0 3.0 %collective-permute-start.31 = (f16[2,192,128]{2,1,0:T(8,128)(2,1)S(1)}, f16[2,192,128]{2,1,0:T(8,128)(2,1)S(1)}, u32[]{:S(2)}, u32[]{:S(2)}) collective-permute-start(f16[2,192,128]{2,1,0:T(8,128)(2,1)S(1)} %get-tuple-element.93), channel_id=1, source_target_pairs={{0,14},{2,12},{4,10},{6,8},{8,6},{10,4},{12,2},{14,0},{1,15},{3,13... | collective-permute-start | bytes 294920 | tf_op jit(solution)/shard_map/ppermute | solution.py:732
  85.0 1.4 %collective-permute-start.30 = (f16[2,192,128]{2,1,0:T(8,128)(2,1)S(1)}, f16[2,192,128]{2,1,0:T(8,128)(2,1)S(1)}, u32[]{:S(2)}, u32[]{:S(2)}) collective-permute-start(f16[2,192,128]{2,1,0:T(8,128)(2,1)S(1)} %get-tuple-element.94), channel_id=1, source_target_pairs={{0,12},{2,14},{4,8},{6,10},{8,4},{10,6},{12,0},{14,2},{1,13},{3,15... | collective-permute-start | bytes 294920 | tf_op jit(solution)/shard_map/ppermute | solution.py:732
  86.4 1.7 %collective-permute-start.29 = (f16[2,192,128]{2,1,0:T(8,128)(2,1)S(1)}, f16[2,192,128]{2,1,0:T(8,128)(2,1)S(1)}, u32[]{:S(2)}, u32[]{:S(2)}) collective-permute-start(f16[2,192,128]{2,1,0:T(8,128)(2,1)S(1)} %get-tuple-element.95), channel_id=1, source_target_pairs={{0,10},{2,8},{4,14},{6,12},{8,2},{10,0},{12,6},{14,4},{1,11},{3,9}... | collective-permute-start | bytes 294920 | tf_op jit(solution)/shard_map/ppermute | solution.py:732
  88.1 1.6 %collective-permute-start.28 = (f16[2,192,128]{2,1,0:T(8,128)(2,1)S(1)}, f16[2,192,128]{2,1,0:T(8,128)(2,1)S(1)}, u32[]{:S(2)}, u32[]{:S(2)}) collective-permute-start(f16[2,192,128]{2,1,0:T(8,128)(2,1)S(1)} %get-tuple-element.96), channel_id=1, source_target_pairs={{0,8},{2,10},{4,12},{6,14},{8,0},{10,2},{12,4},{14,6},{1,9},{3,11}... | collective-permute-start | bytes 294920 | tf_op jit(solution)/shard_map/ppermute | solution.py:732
  89.7 1.3 %collective-permute-start.27 = (f16[2,192,128]{2,1,0:T(8,128)(2,1)S(1)}, f16[2,192,128]{2,1,0:T(8,128)(2,1)S(1)}, u32[]{:S(2)}, u32[]{:S(2)}) collective-permute-start(f16[2,192,128]{2,1,0:T(8,128)(2,1)S(1)} %get-tuple-element.97), channel_id=1, source_target_pairs={{0,6},{2,4},{4,2},{6,0},{8,14},{10,12},{12,10},{14,8},{1,7},{3,5},... | collective-permute-start | bytes 294920 | tf_op jit(solution)/shard_map/ppermute | solution.py:732
  91.1 3.9 %rows_both_ways.3 = f32[8,2,192,128]{3,2,1,0:T(8,128)S(1)} custom-call(s32[2]{0:T(128)S(1)} %pad_add_fusion.first.token.place, f32[8,2,192,128]{3,2,1,0:T(8,128)S(1)} %convert_dynamic-update-slice_fusion.14.data, f32[8,96,128]{2,1,0:T(8,128)S(1)} %get-tuple-element.64.kept, f32[2,8,384,128]{3,2,1,0:T(8,128)S(1)} %get-tuple-element.65.target, ...), custom_call_target="tpu_custom_call" | custom-call | flops 603979776 | bytes 6291456 | tf_op jit(solution)/shard_map/rows_both_ways/pallas_call | solution.py:535
  95.1 0.2 convert.67
  95.4 3.0 %collective-permute-start.26 = (f16[2,192,128]{2,1,0:T(8,128)(2,1)S(1)}, f16[2,192,128]{2,1,0:T(8,128)(2,1)S(1)}, u32[]{:S(2)}, u32[]{:S(2)}) collective-permute-start(f16[2,192,128]{2,1,0:T(8,128)(2,1)S(1)} %get-tuple-element.98), channel_id=1, source_target_pairs={{0,4},{2,6},{4,0},{6,2},{8,12},{10,14},{12,8},{14,10},{1,5},{3,7},... | collective-permute-start | bytes 294920 | tf_op jit(solution)/shard_map/ppermute | solution.py:732
  98.4 1.1 collective-permute-start.25
  99.6 2.5 %collective-permute-done.29 = f16[2,192,128]{2,1,0:T(8,128)(2,1)S(1)} collective-permute-done((f16[2,192,128]{2,1,0:T(8,128)(2,1)S(1)}, f16[2,192,128]{2,1,0:T(8,128)(2,1)S(1)}, u32[]{:S(2)}, u32[]{:S(2)}) %collective-permute-start.29) | collective-permute-done | bytes 98336 | tf_op jit(solution)/shard_map/ppermute | solution.py:732
  102.0 1.7 %collective-permute-start.24 = (f16[2,192,128]{2,1,0:T(8,128)(2,1)S(1)}, f16[2,192,128]{2,1,0:T(8,128)(2,1)S(1)}, u32[]{:S(2)}, u32[]{:S(2)}) collective-permute-start(f16[2,192,128]{2,1,0:T(8,128)(2,1)S(1)} %get-tuple-element.100), channel_id=1, source_target_pairs={{0,14},{2,12},{4,10},{6,8},{8,6},{10,4},{12,2},{14,0},{1,15},{3,13... | collective-permute-start | bytes 294920 | tf_op jit(solution)/shard_map/ppermute | solution.py:732
  103.8 4.4 %collective-permute-done.28 = f16[2,192,128]{2,1,0:T(8,128)(2,1)S(1)} collective-permute-done((f16[2,192,128]{2,1,0:T(8,128)(2,1)S(1)}, f16[2,192,128]{2,1,0:T(8,128)(2,1)S(1)}, u32[]{:S(2)}, u32[]{:S(2)}) %collective-permute-start.28) | collective-permute-done | bytes 98336 | tf_op jit(solution)/shard_map/ppermute | solution.py:732
  108.2 3.2 %collective-permute-start.21 = (f16[2,192,128]{2,1,0:T(8,128)(2,1)S(1)}, f16[2,192,128]{2,1,0:T(8,128)(2,1)S(1)}, u32[]{:S(2)}, u32[]{:S(2)}) collective-permute-start(f16[2,192,128]{2,1,0:T(8,128)(2,1)S(1)} %get-tuple-element.103), channel_id=1, source_target_pairs={{0,8},{2,10},{4,12},{6,14},{8,0},{10,2},{12,4},{14,6},{1,9},{3,11}... | collective-permute-start | bytes 294920 | tf_op jit(solution)/shard_map/ppermute | solution.py:732
  111.5 2.1 %collective-permute-start.20 = (f16[2,192,128]{2,1,0:T(8,128)(2,1)S(1)}, f16[2,192,128]{2,1,0:T(8,128)(2,1)S(1)}, u32[]{:S(2)}, u32[]{:S(2)}) collective-permute-start(f16[2,192,128]{2,1,0:T(8,128)(2,1)S(1)} %get-tuple-element.104), channel_id=1, source_target_pairs={{0,6},{2,4},{4,2},{6,0},{8,14},{10,12},{12,10},{14,8},{1,7},{3,5},... | collective-permute-start | bytes 294920 | tf_op jit(solution)/shard_map/ppermute | solution.py:732
  113.8 0.6 collective-permute-start.19
  114.3 0.4 collective-permute-done.23
  114.7 0.9 collective-permute-start.18
  115.6 2.4 %columns_inverse.2.refs_0_ = f32[2,128,768]{2,1,0:T(8,128)S(1)} custom-call(s32[2]{0:T(128)S(1)} %pad_add_fusion.first.token.place, f32[8,2,2,3,32,128]{5,4,3,2,1,0:T(8,128)S(1)} %convert_dynamic-update-slice_fusion.7.data, f32[4,2,128,768]{3,2,1,0:T(8,128)S(1)} %copy-done.1, f32[8,128]{1,0:T(8,128)S(1)} %get-tuple-element.53.scales, ...), custom_call_target="tpu_custom_call" | custom-call | flops 1207959552 | bytes 3145728 | tf_op jit(solution)/shard_map/columns_inverse/pallas_call | solution.py:624
  118.0 0.4 collective-permute-done.21
  118.5 0.7 collective-permute-done.19
  119.2 0.2 collective-permute-done.18
  119.6 2.5 %columns_inverse.3 = (f32[2,128,384]{2,1,0:T(8,128)S(1)}, f32[2,128,384]{2,1,0:T(8,128)S(1)}) custom-call(s32[2]{0:T(128)S(1)} %pad_add_fusion.first.token.place, f32[8,2,2,3,32,128]{5,4,3,2,1,0:T(8,128)S(1)} %convert_dynamic-update-slice_fusion.data, f32[4,2,128,768]{3,2,1,0:T(8,128)S(1)} %copy-done.1, f32[8,128]{1,0:T(8,128)S(1)} %get-tuple-element.53.scales, ...), custom_call_target="tpu_custom_call" | custom-call | flops 1207959552 | bytes 3145728 | tf_op jit(solution)/shard_map/columns_inverse/pallas_call | solution.py:624
  122.2 1.7 %collective-permute-done.32 = f32[2,128,384]{2,1,0:T(8,128)S(1)} collective-permute-done((f32[2,128,384]{2,1,0:T(8,128)S(1)}, f32[2,128,384]{2,1,0:T(8,128)S(1)}, u32[]{:S(2)}, u32[]{:S(2)}) %collective-permute-start.32) | collective-permute-done | bytes 393248 | tf_op jit(solution)/shard_map/ppermute | solution.py:328
  123.9 0.9 multiply_add_fusion
  (97 shorter events, 1.7 us)
Async XLA Ops:
  1.1 1.5 %collective-permute-start = (f32[2,128,8]{2,1,0:T(8,128)S(1)}, f32[2,128,8]{2,1,0:T(8,128)S(1)}, u32[]{:S(2)}, u32[]{:S(2)}) collective-permute-start(f32[2,128,8]{2,1,0:T(8,128)S(1)} %slice_select_fusion), channel_id=1, source_target_pairs={{0,1},{1,0},{2,3},{3,2},{4,5},{5,4},{6,7},{7,6},{8,9},{9,8},{10,11... | collective-permute-start | bytes 24584 | tf_op jit(solution)/shard_map/ppermute | solution.py:328
  2.6 9.9 %collective-permute-start.1 = (f32[2,8,392]{2,1,0:T(8,128)S(1)}, f32[2,8,392]{2,1,0:T(8,128)S(1)}, u32[]{:S(2)}, u32[]{:S(2)}) collective-permute-start(f32[2,8,392]{2,1,0:T(8,128)S(1)} %pad_maximum_fusion), channel_id=1, source_target_pairs={{0,2},{2,4},{4,6},{6,8},{8,10},{10,12},{12,14},{1,3},{3,5},{5,7},{... | collective-permute-start | bytes 75272 | tf_op jit(solution)/shard_map/ppermute | solution.py:321
  7.4 5.8 %collective-permute-start.2 = (f32[2,8,392]{2,1,0:T(8,128)S(1)}, f32[2,8,392]{2,1,0:T(8,128)S(1)}, u32[]{:S(2)}, u32[]{:S(2)}) collective-permute-start(f32[2,8,392]{2,1,0:T(8,128)S(1)} %pad_maximum_fusion.1), channel_id=1, source_target_pairs={{2,0},{4,2},{6,4},{8,6},{10,8},{12,10},{14,12},{3,1},{5,3},{7,5},{... | collective-permute-start | bytes 75272 | tf_op jit(solution)/shard_map/ppermute | solution.py:322
  8.8 1.1 copy-start.8
  9.9 0.9 copy-start.10
  10.8 0.7 copy-start.13
  11.5 0.7 copy-start.14
  13.2 1.0 copy-start.9
  14.2 21.1 %copy-start.1 = (f32[4,2,128,768]{3,2,1,0:T(8,128)S(1)}, f32[4,2,128,768]{3,2,1,0:T(8,128)}, u32[]{:S(2)}) copy-start(f32[4,2,128,768]{3,2,1,0:T(8,128)} %maps.7) | copy-start | bytes 9437188
  14.2 21.1 %copy-start.3 = (bf16[2,512,512]{2,1,0:T(8,128)(2,1)S(1)}, bf16[2,512,512]{2,1,0:T(8,128)(2,1)}, u32[]{:S(2)}) copy-start(bf16[2,512,512]{2,1,0:T(8,128)(2,1)} %constant.33.clone.matrix) | copy-start | bytes 3145732
  14.2 21.1 %copy-start.11 = (f32[2,3,256]{2,1,0:T(4,128)S(1)}, f32[2,3,256]{2,1,0:T(4,128)}, u32[]{:S(2)}) copy-start(f32[2,3,256]{2,1,0:T(4,128)} %constant.34.clone.table) | copy-start | bytes 18436
  33.6 1.8 %collective-permute-start.3 = (f32[2,128,384]{2,1,0:T(8,128)S(1)}, f32[2,128,384]{2,1,0:T(8,128)S(1)}, u32[]{:S(2)}, u32[]{:S(2)}) collective-permute-start(f32[2,128,384]{2,1,0:T(8,128)S(1)} %get-tuple-element.52.mine), channel_id=1, source_target_pairs={{0,1},{1,0},{2,3},{3,2},{4,5},{5,4},{6,7},{7,6},{8,9},{9,8},{10,11... | collective-permute-start | bytes 1179656 | tf_op jit(solution)/shard_map/ppermute | solution.py:328
  37.8 2.6 %copy-start.5 = (f32[8,2,2,3,32,128]{5,4,3,2,1,0:T(8,128)}, f32[8,2,2,3,32,128]{5,4,3,2,1,0:T(8,128)S(1)}, u32[]{:S(2)}) copy-start(f32[8,2,2,3,32,128]{5,4,3,2,1,0:T(8,128)S(1)} %columns_forward.2) | copy-start | bytes 4718596
  40.5 1.2 copy-start.4
  40.5 11.5 %copy-start = (f32[2,96,4,1024]{3,2,1,0:T(4,128)S(1)}, f32[2,96,4,1024]{3,2,1,0:T(4,128)}, u32[]{:S(2)}) copy-start(f32[2,96,4,1024]{3,2,1,0:T(4,128)} %refs_7_.1) | copy-start | bytes 9437188
  40.5 11.5 %copy-start.2 = (s32[96,1024]{1,0:T(8,128)S(1)}, s32[96,1024]{1,0:T(8,128)}, u32[]{:S(2)}) copy-start(s32[96,1024]{1,0:T(8,128)} %refs_15_.1) | copy-start | bytes 1179652
  41.7 16.0 %collective-permute-start.16 = (f16[2,192,128]{2,1,0:T(8,128)(2,1)S(1)}, f16[2,192,128]{2,1,0:T(8,128)(2,1)S(1)}, u32[]{:S(2)}, u32[]{:S(2)}) collective-permute-start(f16[2,192,128]{2,1,0:T(8,128)(2,1)S(1)} %bitcast.164), channel_id=1, source_target_pairs={{0,12},{2,14},{4,8},{6,10},{8,4},{10,6},{12,0},{14,2},{1,13},{3,15... | collective-permute-start | bytes 294920 | tf_op jit(solution)/shard_map/ppermute | solution.py:732
  46.6 12.4 %collective-permute-start.17 = (f16[2,192,128]{2,1,0:T(8,128)(2,1)S(1)}, f16[2,192,128]{2,1,0:T(8,128)(2,1)S(1)}, u32[]{:S(2)}, u32[]{:S(2)}) collective-permute-start(f16[2,192,128]{2,1,0:T(8,128)(2,1)S(1)} %bitcast.163), channel_id=1, source_target_pairs={{0,14},{2,12},{4,10},{6,8},{8,6},{10,4},{12,2},{14,0},{1,15},{3,13... | collective-permute-start | bytes 294920 | tf_op jit(solution)/shard_map/ppermute | solution.py:732
  47.3 15.6 %collective-permute-start.15 = (f16[2,192,128]{2,1,0:T(8,128)(2,1)S(1)}, f16[2,192,128]{2,1,0:T(8,128)(2,1)S(1)}, u32[]{:S(2)}, u32[]{:S(2)}) collective-permute-start(f16[2,192,128]{2,1,0:T(8,128)(2,1)S(1)} %bitcast.162), channel_id=1, source_target_pairs={{0,10},{2,8},{4,14},{6,12},{8,2},{10,0},{12,6},{14,4},{1,11},{3,9}... | collective-permute-start | bytes 294920 | tf_op jit(solution)/shard_map/ppermute | solution.py:732
  48.5 16.9 %collective-permute-start.14 = (f16[2,192,128]{2,1,0:T(8,128)(2,1)S(1)}, f16[2,192,128]{2,1,0:T(8,128)(2,1)S(1)}, u32[]{:S(2)}, u32[]{:S(2)}) collective-permute-start(f16[2,192,128]{2,1,0:T(8,128)(2,1)S(1)} %bitcast.161), channel_id=1, source_target_pairs={{0,8},{2,10},{4,12},{6,14},{8,0},{10,2},{12,4},{14,6},{1,9},{3,11}... | collective-permute-start | bytes 294920 | tf_op jit(solution)/shard_map/ppermute | solution.py:732
  50.4 16.8 %collective-permute-start.13 = (f16[2,192,128]{2,1,0:T(8,128)(2,1)S(1)}, f16[2,192,128]{2,1,0:T(8,128)(2,1)S(1)}, u32[]{:S(2)}, u32[]{:S(2)}) collective-permute-start(f16[2,192,128]{2,1,0:T(8,128)(2,1)S(1)} %bitcast.160), channel_id=1, source_target_pairs={{0,6},{2,4},{4,2},{6,0},{8,14},{10,12},{12,10},{14,8},{1,7},{3,5},... | collective-permute-start | bytes 294920 | tf_op jit(solution)/shard_map/ppermute | solution.py:732
  52.0 19.2 %slice-start.1 = ((f32[8,2,2,3,32,128]{5,4,3,2,1,0:T(8,128)}), f32[1,2,2,3,32,128]{5,4,3,2,1,0:T(8,128)S(1)}, s32[]{:S(2)}) async-start(f32[8,2,2,3,32,128]{5,4,3,2,1,0:T(8,128)} %copy-done.5), calls=%async_computation.1 | async-start | bytes 393216 | tf_op jit(solution)/shard_map/slice | solution.py:731
  57.7 9.5 %collective-permute-start.12 = (f16[2,192,128]{2,1,0:T(8,128)(2,1)S(1)}, f16[2,192,128]{2,1,0:T(8,128)(2,1)S(1)}, u32[]{:S(2)}, u32[]{:S(2)}) collective-permute-start(f16[2,192,128]{2,1,0:T(8,128)(2,1)S(1)} %bitcast.159), channel_id=1, source_target_pairs={{0,4},{2,6},{4,0},{6,2},{8,12},{10,14},{12,8},{14,10},{1,5},{3,7},... | collective-permute-start | bytes 294920 | tf_op jit(solution)/shard_map/ppermute | solution.py:732
  59.0 11.7 %collective-permute-start.11 = (f16[2,192,128]{2,1,0:T(8,128)(2,1)S(1)}, f16[2,192,128]{2,1,0:T(8,128)(2,1)S(1)}, u32[]{:S(2)}, u32[]{:S(2)}) collective-permute-start(f16[2,192,128]{2,1,0:T(8,128)(2,1)S(1)} %bitcast.158), channel_id=1, source_target_pairs={{0,2},{2,0},{4,6},{6,4},{8,10},{10,8},{12,14},{14,12},{1,3},{3,1},... | collective-permute-start | bytes 294920 | tf_op jit(solution)/shard_map/ppermute | solution.py:732
  59.8 11.5 %copy-start.6 = (bf16[2,256,256]{2,1,0:T(8,128)(2,1)S(1)}, bf16[2,256,256]{2,1,0:T(8,128)(2,1)}, u32[]{:S(2)}) copy-start(bf16[2,256,256]{2,1,0:T(8,128)(2,1)} %constant.36.clone.inverse) | copy-start | bytes 786436
  59.8 11.5 %copy-start.7 = (bf16[2,256,256]{2,1,0:T(8,128)(2,1)S(1)}, bf16[2,256,256]{2,1,0:T(8,128)(2,1)}, u32[]{:S(2)}) copy-start(bf16[2,256,256]{2,1,0:T(8,128)(2,1)} %constant.35.clone.forward) | copy-start | bytes 786436
  59.9 11.5 %copy-start.12 = (f32[2,8,128]{2,1,0:T(8,128)S(1)}, f32[2,8,128]{2,1,0:T(8,128)}, u32[]{:S(2)}) copy-start(f32[2,8,128]{2,1,0:T(8,128)} %constant.37.clone.table) | copy-start | bytes 24580
  62.9 12.5 %collective-permute-start.9 = (f16[2,192,128]{2,1,0:T(8,128)(2,1)S(1)}, f16[2,192,128]{2,1,0:T(8,128)(2,1)S(1)}, u32[]{:S(2)}, u32[]{:S(2)}) collective-permute-start(f16[2,192,128]{2,1,0:T(8,128)(2,1)S(1)} %bitcast.157), channel_id=1, source_target_pairs={{0,12},{2,14},{4,8},{6,10},{8,4},{10,6},{12,0},{14,2},{1,13},{3,15... | collective-permute-start | bytes 294920 | tf_op jit(solution)/shard_map/ppermute | solution.py:732
  65.4 12.0 %collective-permute-start.10 = (f16[2,192,128]{2,1,0:T(8,128)(2,1)S(1)}, f16[2,192,128]{2,1,0:T(8,128)(2,1)S(1)}, u32[]{:S(2)}, u32[]{:S(2)}) collective-permute-start(f16[2,192,128]{2,1,0:T(8,128)(2,1)S(1)} %bitcast.156), channel_id=1, source_target_pairs={{0,14},{2,12},{4,10},{6,8},{8,6},{10,4},{12,2},{14,0},{1,15},{3,13... | collective-permute-start | bytes 294920 | tf_op jit(solution)/shard_map/ppermute | solution.py:732
  67.2 13.0 %collective-permute-start.8 = (f16[2,192,128]{2,1,0:T(8,128)(2,1)S(1)}, f16[2,192,128]{2,1,0:T(8,128)(2,1)S(1)}, u32[]{:S(2)}, u32[]{:S(2)}) collective-permute-start(f16[2,192,128]{2,1,0:T(8,128)(2,1)S(1)} %bitcast.155), channel_id=1, source_target_pairs={{0,10},{2,8},{4,14},{6,12},{8,2},{10,0},{12,6},{14,4},{1,11},{3,9}... | collective-permute-start | bytes 294920 | tf_op jit(solution)/shard_map/ppermute | solution.py:732
  67.2 13.8 %collective-permute-start.7 = (f16[2,192,128]{2,1,0:T(8,128)(2,1)S(1)}, f16[2,192,128]{2,1,0:T(8,128)(2,1)S(1)}, u32[]{:S(2)}, u32[]{:S(2)}) collective-permute-start(f16[2,192,128]{2,1,0:T(8,128)(2,1)S(1)} %bitcast.154), channel_id=1, source_target_pairs={{0,8},{2,10},{4,12},{6,14},{8,0},{10,2},{12,4},{14,6},{1,9},{3,11}... | collective-permute-start | bytes 294920 | tf_op jit(solution)/shard_map/ppermute | solution.py:732
  70.7 10.4 %collective-permute-start.6 = (f16[2,192,128]{2,1,0:T(8,128)(2,1)S(1)}, f16[2,192,128]{2,1,0:T(8,128)(2,1)S(1)}, u32[]{:S(2)}, u32[]{:S(2)}) collective-permute-start(f16[2,192,128]{2,1,0:T(8,128)(2,1)S(1)} %bitcast.153), channel_id=1, source_target_pairs={{0,6},{2,4},{4,2},{6,0},{8,14},{10,12},{12,10},{14,8},{1,7},{3,5},... | collective-permute-start | bytes 294920 | tf_op jit(solution)/shard_map/ppermute | solution.py:732
  75.1 15.8 %slice-start = ((f32[8,2,2,3,32,128]{5,4,3,2,1,0:T(8,128)}), f32[1,2,2,3,32,128]{5,4,3,2,1,0:T(8,128)S(1)}, s32[]{:S(2)}) async-start(f32[8,2,2,3,32,128]{5,4,3,2,1,0:T(8,128)} %copy-done.4), calls=%async_computation | async-start | bytes 393216 | tf_op jit(solution)/shard_map/slice | solution.py:731
  75.5 6.5 %collective-permute-start.5 = (f16[2,192,128]{2,1,0:T(8,128)(2,1)S(1)}, f16[2,192,128]{2,1,0:T(8,128)(2,1)S(1)}, u32[]{:S(2)}, u32[]{:S(2)}) collective-permute-start(f16[2,192,128]{2,1,0:T(8,128)(2,1)S(1)} %bitcast.152), channel_id=1, source_target_pairs={{0,4},{2,6},{4,0},{6,2},{8,12},{10,14},{12,8},{14,10},{1,5},{3,7},... | collective-permute-start | bytes 294920 | tf_op jit(solution)/shard_map/ppermute | solution.py:732
  77.4 4.6 %collective-permute-start.4 = (f16[2,192,128]{2,1,0:T(8,128)(2,1)S(1)}, f16[2,192,128]{2,1,0:T(8,128)(2,1)S(1)}, u32[]{:S(2)}, u32[]{:S(2)}) collective-permute-start(f16[2,192,128]{2,1,0:T(8,128)(2,1)S(1)} %bitcast.151), channel_id=1, source_target_pairs={{0,2},{2,0},{4,6},{6,4},{8,10},{10,8},{12,14},{14,12},{1,3},{3,1},... | collective-permute-start | bytes 294920 | tf_op jit(solution)/shard_map/ppermute | solution.py:732
  82.0 13.3 %collective-permute-start.31 = (f16[2,192,128]{2,1,0:T(8,128)(2,1)S(1)}, f16[2,192,128]{2,1,0:T(8,128)(2,1)S(1)}, u32[]{:S(2)}, u32[]{:S(2)}) collective-permute-start(f16[2,192,128]{2,1,0:T(8,128)(2,1)S(1)} %get-tuple-element.93), channel_id=1, source_target_pairs={{0,14},{2,12},{4,10},{6,8},{8,6},{10,4},{12,2},{14,0},{1,15},{3,13... | collective-permute-start | bytes 294920 | tf_op jit(solution)/shard_map/ppermute | solution.py:732
  85.0 13.4 %collective-permute-start.30 = (f16[2,192,128]{2,1,0:T(8,128)(2,1)S(1)}, f16[2,192,128]{2,1,0:T(8,128)(2,1)S(1)}, u32[]{:S(2)}, u32[]{:S(2)}) collective-permute-start(f16[2,192,128]{2,1,0:T(8,128)(2,1)S(1)} %get-tuple-element.94), channel_id=1, source_target_pairs={{0,12},{2,14},{4,8},{6,10},{8,4},{10,6},{12,0},{14,2},{1,13},{3,15... | collective-permute-start | bytes 294920 | tf_op jit(solution)/shard_map/ppermute | solution.py:732
  86.4 15.6 %collective-permute-start.29 = (f16[2,192,128]{2,1,0:T(8,128)(2,1)S(1)}, f16[2,192,128]{2,1,0:T(8,128)(2,1)S(1)}, u32[]{:S(2)}, u32[]{:S(2)}) collective-permute-start(f16[2,192,128]{2,1,0:T(8,128)(2,1)S(1)} %get-tuple-element.95), channel_id=1, source_target_pairs={{0,10},{2,8},{4,14},{6,12},{8,2},{10,0},{12,6},{14,4},{1,11},{3,9}... | collective-permute-start | bytes 294920 | tf_op jit(solution)/shard_map/ppermute | solution.py:732
  88.1 20.1 %collective-permute-start.28 = (f16[2,192,128]{2,1,0:T(8,128)(2,1)S(1)}, f16[2,192,128]{2,1,0:T(8,128)(2,1)S(1)}, u32[]{:S(2)}, u32[]{:S(2)}) collective-permute-start(f16[2,192,128]{2,1,0:T(8,128)(2,1)S(1)} %get-tuple-element.96), channel_id=1, source_target_pairs={{0,8},{2,10},{4,12},{6,14},{8,0},{10,2},{12,4},{14,6},{1,9},{3,11}... | collective-permute-start | bytes 294920 | tf_op jit(solution)/shard_map/ppermute | solution.py:732
  89.7 18.5 %collective-permute-start.27 = (f16[2,192,128]{2,1,0:T(8,128)(2,1)S(1)}, f16[2,192,128]{2,1,0:T(8,128)(2,1)S(1)}, u32[]{:S(2)}, u32[]{:S(2)}) collective-permute-start(f16[2,192,128]{2,1,0:T(8,128)(2,1)S(1)} %get-tuple-element.97), channel_id=1, source_target_pairs={{0,6},{2,4},{4,2},{6,0},{8,14},{10,12},{12,10},{14,8},{1,7},{3,5},... | collective-permute-start | bytes 294920 | tf_op jit(solution)/shard_map/ppermute | solution.py:732
  95.4 12.8 %collective-permute-start.26 = (f16[2,192,128]{2,1,0:T(8,128)(2,1)S(1)}, f16[2,192,128]{2,1,0:T(8,128)(2,1)S(1)}, u32[]{:S(2)}, u32[]{:S(2)}) collective-permute-start(f16[2,192,128]{2,1,0:T(8,128)(2,1)S(1)} %get-tuple-element.98), channel_id=1, source_target_pairs={{0,4},{2,6},{4,0},{6,2},{8,12},{10,14},{12,8},{14,10},{1,5},{3,7},... | collective-permute-start | bytes 294920 | tf_op jit(solution)/shard_map/ppermute | solution.py:732
  98.4 13.1 %collective-permute-start.25 = (f16[2,192,128]{2,1,0:T(8,128)(2,1)S(1)}, f16[2,192,128]{2,1,0:T(8,128)(2,1)S(1)}, u32[]{:S(2)}, u32[]{:S(2)}) collective-permute-start(f16[2,192,128]{2,1,0:T(8,128)(2,1)S(1)} %get-tuple-element.99), channel_id=1, source_target_pairs={{0,2},{2,0},{4,6},{6,4},{8,10},{10,8},{12,14},{14,12},{1,3},{3,1},... | collective-permute-start | bytes 294920 | tf_op jit(solution)/shard_map/ppermute | solution.py:732
  102.0 11.7 %collective-permute-start.24 = (f16[2,192,128]{2,1,0:T(8,128)(2,1)S(1)}, f16[2,192,128]{2,1,0:T(8,128)(2,1)S(1)}, u32[]{:S(2)}, u32[]{:S(2)}) collective-permute-start(f16[2,192,128]{2,1,0:T(8,128)(2,1)S(1)} %get-tuple-element.100), channel_id=1, source_target_pairs={{0,14},{2,12},{4,10},{6,8},{8,6},{10,4},{12,2},{14,0},{1,15},{3,13... | collective-permute-start | bytes 294920 | tf_op jit(solution)/shard_map/ppermute | solution.py:732
  108.2 6.5 %collective-permute-start.23 = (f16[2,192,128]{2,1,0:T(8,128)(2,1)S(1)}, f16[2,192,128]{2,1,0:T(8,128)(2,1)S(1)}, u32[]{:S(2)}, u32[]{:S(2)}) collective-permute-start(f16[2,192,128]{2,1,0:T(8,128)(2,1)S(1)} %get-tuple-element.101), channel_id=1, source_target_pairs={{0,12},{2,14},{4,8},{6,10},{8,4},{10,6},{12,0},{14,2},{1,13},{3,15... | collective-permute-start | bytes 294920 | tf_op jit(solution)/shard_map/ppermute | solution.py:732
  108.2 9.8 %collective-permute-start.22 = (f16[2,192,128]{2,1,0:T(8,128)(2,1)S(1)}, f16[2,192,128]{2,1,0:T(8,128)(2,1)S(1)}, u32[]{:S(2)}, u32[]{:S(2)}) collective-permute-start(f16[2,192,128]{2,1,0:T(8,128)(2,1)S(1)} %get-tuple-element.102), channel_id=1, source_target_pairs={{0,10},{2,8},{4,14},{6,12},{8,2},{10,0},{12,6},{14,4},{1,11},{3,9}... | collective-permute-start | bytes 294920 | tf_op jit(solution)/shard_map/ppermute | solution.py:732
  108.2 10.2 %collective-permute-start.21 = (f16[2,192,128]{2,1,0:T(8,128)(2,1)S(1)}, f16[2,192,128]{2,1,0:T(8,128)(2,1)S(1)}, u32[]{:S(2)}, u32[]{:S(2)}) collective-permute-start(f16[2,192,128]{2,1,0:T(8,128)(2,1)S(1)} %get-tuple-element.103), channel_id=1, source_target_pairs={{0,8},{2,10},{4,12},{6,14},{8,0},{10,2},{12,4},{14,6},{1,9},{3,11}... | collective-permute-start | bytes 294920 | tf_op jit(solution)/shard_map/ppermute | solution.py:732
  111.5 7.0 %collective-permute-start.20 = (f16[2,192,128]{2,1,0:T(8,128)(2,1)S(1)}, f16[2,192,128]{2,1,0:T(8,128)(2,1)S(1)}, u32[]{:S(2)}, u32[]{:S(2)}) collective-permute-start(f16[2,192,128]{2,1,0:T(8,128)(2,1)S(1)} %get-tuple-element.104), channel_id=1, source_target_pairs={{0,6},{2,4},{4,2},{6,0},{8,14},{10,12},{12,10},{14,8},{1,7},{3,5},... | collective-permute-start | bytes 294920 | tf_op jit(solution)/shard_map/ppermute | solution.py:732
  113.8 5.4 %collective-permute-start.19 = (f16[2,192,128]{2,1,0:T(8,128)(2,1)S(1)}, f16[2,192,128]{2,1,0:T(8,128)(2,1)S(1)}, u32[]{:S(2)}, u32[]{:S(2)}) collective-permute-start(f16[2,192,128]{2,1,0:T(8,128)(2,1)S(1)} %get-tuple-element.105), channel_id=1, source_target_pairs={{0,4},{2,6},{4,0},{6,2},{8,12},{10,14},{12,8},{14,10},{1,5},{3,7},... | collective-permute-start | bytes 294920 | tf_op jit(solution)/shard_map/ppermute | solution.py:732
  114.7 4.7 %collective-permute-start.18 = (f16[2,192,128]{2,1,0:T(8,128)(2,1)S(1)}, f16[2,192,128]{2,1,0:T(8,128)(2,1)S(1)}, u32[]{:S(2)}, u32[]{:S(2)}) collective-permute-start(f16[2,192,128]{2,1,0:T(8,128)(2,1)S(1)} %get-tuple-element.106), channel_id=1, source_target_pairs={{0,2},{2,0},{4,6},{6,4},{8,10},{10,8},{12,14},{14,12},{1,3},{3,1},... | collective-permute-start | bytes 294920 | tf_op jit(solution)/shard_map/ppermute | solution.py:732
  119.6 4.3 %copy-start.15 = (f32[2,128,384]{2,1,0:T(8,128)S(1)}, f32[2,128,384]{2,1,0:T(8,128)}, u32[]{:S(2)}) copy-start(f32[2,128,384]{2,1,0:T(8,128)} %param.24) | copy-start | bytes 1179652
  122.1 1.8 %collective-permute-start.32 = (f32[2,128,384]{2,1,0:T(8,128)S(1)}, f32[2,128,384]{2,1,0:T(8,128)S(1)}, u32[]{:S(2)}, u32[]{:S(2)}) collective-permute-start(f32[2,128,384]{2,1,0:T(8,128)S(1)} %get-tuple-element.91), channel_id=1, source_target_pairs={{0,1},{1,0},{2,3},{3,2},{4,5},{5,4},{6,7},{7,6},{8,9},{9,8},{10,11... | collective-permute-start | bytes 1179656 | tf_op jit(solution)/shard_map/ppermute | solution.py:328

commit v2 on v1

--- a/solution.py
+++ b/solution.py
@@ -653,23 +653,31 @@
     count, height = lines.shape
     coils = count // pencil
     per = pencil // radix3
+    size = order.shape[0]
+    span = size // radix
+
+    def reordered(value):
+        pieces = [mm(value[:, k : k + size], order[...]) for k in range(0, height, size)]
+        if value.shape[0] > count:
+            pieces = [piece[:count] + piece[count:] for piece in pieces]
+        return [
+            jnp.concatenate([piece[:, q * span : (q + 1) * span] for piece in pieces], axis=1)
+            for q in range(radix)
+        ]
 
     @pl.when(pl.program_id(0) == 0)
     def _():
-        source = lax.broadcasted_iota(jnp.int32, (height, LANES), 0)
-        place = lax.broadcasted_iota(jnp.int32, (height, LANES), 1)
-        for q in range(radix):
-            order[:, q * LANES : (q + 1) * LANES] = jnp.where(
-                source == radix * place + q, 1.0, 0.0
-            ).astype(BF16)
+        source = lax.broadcasted_iota(jnp.int32, order.shape, 0)
+        place = lax.broadcasted_iota(jnp.int32, order.shape, 1)
+        place = radix * lax.rem(place, span) + lax.div(place, span)
+        order[...] = jnp.where(source == place, 1.0, 0.0).astype(BF16)
         for t in range(tiles):
             for q in range(radix3):
                 lines[q * per : (q + 1) * per, t * LANES : (t + 1) * LANES] = sampled[t][
                     pl.ds(q, per, stride=radix3), :
                 ].astype(F32)
-        picked = mm(lines[0:pencil, :].astype(BF16), order[...])
-        for q in range(radix):
-            kept[q] = picked[:, q * LANES : (q + 1) * LANES]
+        for q, part in enumerate(reordered(lines[0:pencil, :].astype(BF16))):
+            kept[q] = part
 
     for t in range(tiles):
         source = measured[t].reshape(count, LANES)
@@ -680,13 +688,8 @@
                     pl.ds(q * coils + c, per, stride=radix3 * coils), :
                 ]
     both = jnp.concatenate(split2(lines[...]), axis=0)
-    for q in range(0, radix, 2):
-        width = min(2, radix - q) * LANES
-        part = order[:, q * LANES : q * LANES + width]
-        picked = mm(both, part)
-        picked = picked[:count] + picked[count:]
-        for k in range(0, width, LANES):
-            target[0, q + k // LANES] = picked[:, k : k + LANES]
+    for q, part in enumerate(reordered(both)):
+        target[0, q] = part
 
 
 def prepare_target(token, measured, sampled, radix3):
@@ -710,7 +713,7 @@
             pl.BlockSpec((1, radix, count, LANES), lambda i: (i, 0, 0, 0)),
             pl.BlockSpec((radix, pencil, LANES), lambda i: (0, 0, 0)),
         ),
-        scratch_shapes=[pltpu.VMEM((count, height), F32), pltpu.VMEM((height, height), BF16)],
+        scratch_shapes=[pltpu.VMEM((count, height), F32), pltpu.VMEM((INNER, INNER), BF16)],
         cost_estimate=pl.CostEstimate(
             flops=8 * count * height * height, bytes_accessed=16 * count * height, transcendentals=0
         ),
@@ -728,10 +731,11 @@
     if not pairwise(groups):
         value = value.astype(jnp.float16)
         return [lax.all_to_all(value, "gz", split_axis=0, concat_axis=0, tiled=True)]
-    return [value[0]] + [
-        lax.ppermute(value[k].astype(jnp.float16), "gz", [(i, i ^ k) for i in range(groups)])
-        for k in range(1, groups)
-    ]
+    blocks = [value[0]]
+    for k in range(1, groups):
+        half = value[k].astype(jnp.float16)
+        blocks.append(lax.ppermute(half, "gz", [(i, i ^ k) for i in range(groups)]))
+    return blocks
 
 
 def receive(parts):
@@ -777,7 +781,7 @@
 
     back = []
     for chunk in range(chunks):
-        lines = receive(after(arrived[chunk], token))
+        lines = receive(arrived[chunk])
         if rows != LANES:
             lines = jnp.transpose(lines, (1, 2, 0, 3)).reshape(2, -1, row_radix, LANES)
             lines = jnp.transpose(lines, (2, 0, 1, 3))

time: 125 us -> 129 us (1.032)
  starting transfers between devices: 51.9 us -> 68.3 us
  waiting for transfers between devices: 19.5 us -> 7.96 us
    ppermute x28, starting transfers between devices: 45.1 us -> 61.5 us  [send(): blocks.append(lax.ppermute(half, 'gz', [(i, i ^ k) for i in range(groups)]))]
    ppermute x28, waiting for transfers between devices: 15.3 us -> 5.33 us  [send(): blocks.append(lax.ppermute(half, 'gz', [(i, i ^ k) for i in range(groups)]))]
    ppermute x3, waiting for transfers between devices: 3.56 us -> 1.94 us  [swap_cores(): return lax.ppermute(value, 'col', [(0, 1), (1, 0)])]
  transfers between devices with their start and end apart: 33 -> 33, of which waited for: 15 -> 8; matrix products, arithmetic and copies ran while one was open for 2% -> 2% of each run, Pallas kernels for 13% -> 12%
where the time goes in v2:
time: 129 us; the launch traced here: 128 us
  starting transfers between devices  68.3 us (53%)
  Pallas kernels  41.6 us (32%)
  waiting for transfers between devices  7.96 us (6%)
  local copies, waits for them, and re-layouts  6.71 us (5%)
  other arithmetic  3.26 us (3%)
    ppermute x28, starting transfers between devices, send(): blocks.append(lax.ppermute(half, 'gz', [(i, i ^ k) for i in range(groups)]))  61.5 us
    pallas_call x1, Pallas kernels, run_network(): pl.pallas_call(network_kernel, out_shape=(shape, shape), in_specs=[pl.Blo...  19.3 us
    pallas_call x2, Pallas kernels, rows_both_ways(): pl.pallas_call(rows_kernel, out_shape=jax.ShapeDtypeStruct(data.shape, F3...  7.62 us
    ppermute x28, waiting for transfers between devices, send(): blocks.append(lax.ppermute(half, 'gz', [(i, i ^ k) for i in range(groups)]))  5.33 us
    unnamed x36, local copies, waits for them, and re-layouts  5.23 us
    pallas_call x1, Pallas kernels, prepare_target(): pl.pallas_call(partial(target_kernel, radix3), out_shape=(jax.ShapeDtypeS...  4.89 us
    ppermute x1, starting transfers between devices, halo(): top = lax.ppermute(lower, 'gz', down)  4.77 us
    pallas_call x2, Pallas kernels, columns_inverse(): pl.pallas_call(partial(columns_inverse_kernel, last), out_shape=shape, gr...  4.75 us
  transfers between devices with their start and end apart: 33, of which 8 were waited for; matrix products, arithmetic and copies ran while one was open for 2% of the time, Pallas kernels for 12%

profile of v2, /device:TPU:0, one launch (start us, length us, event | category | flops | bytes accessed | tf_op | source)
XLA Modules:
  0.0 128.5 jit_solution(8438329410288407724)
XLA Ops:
  0.0 1.1 slice_select_fusion
  1.1 0.6 collective-permute-start
  1.6 0.8 fusion.2
  2.4 0.2 collective-permute-done.side
  2.6 4.8 %collective-permute-start.1 = (f32[2,8,392]{2,1,0:T(8,128)S(1)}, f32[2,8,392]{2,1,0:T(8,128)S(1)}, u32[]{:S(2)}, u32[]{:S(2)}) collective-permute-start(f32[2,8,392]{2,1,0:T(8,128)S(1)} %pad_maximum_fusion), channel_id=1, source_target_pairs={{0,2},{2,4},{4,6},{6,8},{8,10},{10,12},{12,14},{1,3},{3,5},{5,7},{... | collective-permute-start | bytes 75272 | tf_op jit(solution)/shard_map/ppermute | solution.py:321
  7.4 1.3 %collective-permute-start.2 = (f32[2,8,392]{2,1,0:T(8,128)S(1)}, f32[2,8,392]{2,1,0:T(8,128)S(1)}, u32[]{:S(2)}, u32[]{:S(2)}) collective-permute-start(f32[2,8,392]{2,1,0:T(8,128)S(1)} %pad_maximum_fusion.1), channel_id=1, source_target_pairs={{2,0},{4,2},{6,4},{8,6},{10,8},{12,10},{14,12},{3,1},{5,3},{7,5},{... | collective-permute-start | bytes 75272 | tf_op jit(solution)/shard_map/ppermute | solution.py:322
  8.7 0.1 add_convert_fusion.flags
  8.8 1.1 copy-done.8
  9.9 0.9 copy-done.10
  10.8 0.7 copy-done.13
  11.5 0.7 copy-done.14
  12.1 0.4 weights.1
  12.5 0.7 collective-permute-done.2.bottom
  13.2 1.0 copy-done.9
  14.2 19.3 %network.1 = (f32[2,128,384]{2,1,0:T(8,128)S(1)}, f32[2,128,384]{2,1,0:T(8,128)S(1)}) custom-call(s32[4]{0:T(128)S(1)} %add_convert_fusion.flags, f32[2,8,392]{2,1,0:T(8,128)S(1)} %collective-permute-done.1.top, f32[2,128,384]{2,1,0:T(8,128)S(1)} %copy-done.9, f32[2,8,392]{2,1,0:T(8,128)S(1)} %collective-permute-done.2.bottom, ...), custom_call_target="tpu_custom_call" | custom-call | flops 4026531840 | bytes 1179648 | tf_op jit(solution)/shard_map/network/pallas_call | solution.py:292
  33.7 0.1 pad_add_fusion.first.token.place
  33.8 4.9 %target.1 = (f32[2,8,384,128]{3,2,1,0:T(8,128)S(1)}, f32[8,96,128]{2,1,0:T(8,128)S(1)}) custom-call(s32[2]{0:T(128)S(1)} %pad_add_fusion.first.token.place, f32[2,96,4,1024]{3,2,1,0:T(4,128)S(1)} %copy-done, f32[2,96,4,1024]{3,2,1,0:T(4,128)S(1)} %copy-done, f32[2,96,4,1024]{3,2,1,0:T(4,128)S(1)} %copy-done, f32[2,96,4,1024]{3,2,1,0:T(4,128)S(1)} %copy-done, ...), custom_call_target="tpu_custom_call" | custom-call | flops 3221225472 | bytes 6291456 | tf_op jit(solution)/shard_map/target/pallas_call | solution.py:699
  38.7 2.3 %columns_forward.3 = f32[8,2,2,3,32,128]{5,4,3,2,1,0:T(8,128)S(1)} custom-call(s32[2]{0:T(128)S(1)} %pad_add_fusion.first.token.place, f32[2,128,384]{2,1,0:T(8,128)S(1)} %get-tuple-element.34.mine, f32[2,128,384]{2,1,0:T(8,128)S(1)} %collective-permute-done.3.other, f32[4,2,128,768]{3,2,1,0:T(8,128)S(1)} %copy-done.1, ...), custom_call_target="tpu_custom_call" | custom-call | flops 1207959552 | bytes 3145728 | tf_op jit(solution)/shard_map/columns_forward/pallas_call | solution.py:463
  41.0 0.2 convert.67
  41.2 2.3 %columns_forward.2 = f32[8,2,2,3,32,128]{5,4,3,2,1,0:T(8,128)S(1)} custom-call(s32[2]{0:T(128)S(1)} %pad_add_fusion.first.token.place, f32[2,128,384]{2,1,0:T(8,128)S(1)} %get-tuple-element.34.mine, f32[2,128,384]{2,1,0:T(8,128)S(1)} %collective-permute-done.3.other, f32[4,2,128,768]{3,2,1,0:T(8,128)S(1)} %copy-done.1, ...), custom_call_target="tpu_custom_call" | custom-call | flops 1207959552 | bytes 3145728 | tf_op jit(solution)/shard_map/columns_forward/pallas_call | solution.py:463
  43.5 0.2 convert.65
  43.7 0.2 fusion
  43.9 0.8 copy-done.4
  44.7 2.4 %collective-permute-start.18 = (f16[2,192,128]{2,1,0:T(8,128)(2,1)S(1)}, f16[2,192,128]{2,1,0:T(8,128)(2,1)S(1)}, u32[]{:S(2)}, u32[]{:S(2)}) collective-permute-start(f16[2,192,128]{2,1,0:T(8,128)(2,1)S(1)} %bitcast.160), channel_id=1, source_target_pairs={{0,2},{2,0},{4,6},{6,4},{8,10},{10,8},{12,14},{14,12},{1,3},{3,1},... | collective-permute-start | bytes 294920 | tf_op jit(solution)/shard_map/ppermute | solution.py:737
  47.2 1.6 %collective-permute-start.19 = (f16[2,192,128]{2,1,0:T(8,128)(2,1)S(1)}, f16[2,192,128]{2,1,0:T(8,128)(2,1)S(1)}, u32[]{:S(2)}, u32[]{:S(2)}) collective-permute-start(f16[2,192,128]{2,1,0:T(8,128)(2,1)S(1)} %bitcast.159), channel_id=1, source_target_pairs={{0,4},{2,6},{4,0},{6,2},{8,12},{10,14},{12,8},{14,10},{1,5},{3,7},... | collective-permute-start | bytes 294920 | tf_op jit(solution)/shard_map/ppermute | solution.py:737
  48.8 0.4 collective-permute-start.20
  49.3 3.0 %collective-permute-start.21 = (f16[2,192,128]{2,1,0:T(8,128)(2,1)S(1)}, f16[2,192,128]{2,1,0:T(8,128)(2,1)S(1)}, u32[]{:S(2)}, u32[]{:S(2)}) collective-permute-start(f16[2,192,128]{2,1,0:T(8,128)(2,1)S(1)} %bitcast.157), channel_id=1, source_target_pairs={{0,8},{2,10},{4,12},{6,14},{8,0},{10,2},{12,4},{14,6},{1,9},{3,11}... | collective-permute-start | bytes 294920 | tf_op jit(solution)/shard_map/ppermute | solution.py:737
  52.2 0.9 collective-permute-start.22
  53.1 0.2 fusion.1
  53.4 3.2 %collective-permute-start.23 = (f16[2,192,128]{2,1,0:T(8,128)(2,1)S(1)}, f16[2,192,128]{2,1,0:T(8,128)(2,1)S(1)}, u32[]{:S(2)}, u32[]{:S(2)}) collective-permute-start(f16[2,192,128]{2,1,0:T(8,128)(2,1)S(1)} %bitcast.155), channel_id=1, source_target_pairs={{0,12},{2,14},{4,8},{6,10},{8,4},{10,6},{12,0},{14,2},{1,13},{3,15... | collective-permute-start | bytes 294920 | tf_op jit(solution)/shard_map/ppermute | solution.py:737
  56.6 1.5 %collective-permute-start.24 = (f16[2,192,128]{2,1,0:T(8,128)(2,1)S(1)}, f16[2,192,128]{2,1,0:T(8,128)(2,1)S(1)}, u32[]{:S(2)}, u32[]{:S(2)}) collective-permute-start(f16[2,192,128]{2,1,0:T(8,128)(2,1)S(1)} %bitcast.153), channel_id=1, source_target_pairs={{0,14},{2,12},{4,10},{6,8},{8,6},{10,4},{12,2},{14,0},{1,15},{3,13... | collective-permute-start | bytes 294920 | tf_op jit(solution)/shard_map/ppermute | solution.py:737
  58.1 0.8 collective-permute-start.4
  58.9 6.1 %collective-permute-start.5 = (f16[2,192,128]{2,1,0:T(8,128)(2,1)S(1)}, f16[2,192,128]{2,1,0:T(8,128)(2,1)S(1)}, u32[]{:S(2)}, u32[]{:S(2)}) collective-permute-start(f16[2,192,128]{2,1,0:T(8,128)(2,1)S(1)} %bitcast.152), channel_id=1, source_target_pairs={{0,4},{2,6},{4,0},{6,2},{8,12},{10,14},{12,8},{14,10},{1,5},{3,7},... | collective-permute-start | bytes 294920 | tf_op jit(solution)/shard_map/ppermute | solution.py:737
  65.1 2.3 %collective-permute-done.22 = f16[2,192,128]{2,1,0:T(8,128)(2,1)S(1)} collective-permute-done((f16[2,192,128]{2,1,0:T(8,128)(2,1)S(1)}, f16[2,192,128]{2,1,0:T(8,128)(2,1)S(1)}, u32[]{:S(2)}, u32[]{:S(2)}) %collective-permute-start.22) | collective-permute-done | bytes 98336 | tf_op jit(solution)/shard_map/ppermute | solution.py:737
  67.4 4.1 %collective-permute-start.7 = (f16[2,192,128]{2,1,0:T(8,128)(2,1)S(1)}, f16[2,192,128]{2,1,0:T(8,128)(2,1)S(1)}, u32[]{:S(2)}, u32[]{:S(2)}) collective-permute-start(f16[2,192,128]{2,1,0:T(8,128)(2,1)S(1)} %bitcast.150), channel_id=1, source_target_pairs={{0,8},{2,10},{4,12},{6,14},{8,0},{10,2},{12,4},{14,6},{1,9},{3,11}... | collective-permute-start | bytes 294920 | tf_op jit(solution)/shard_map/ppermute | solution.py:737
  71.5 2.8 %collective-permute-start.8 = (f16[2,192,128]{2,1,0:T(8,128)(2,1)S(1)}, f16[2,192,128]{2,1,0:T(8,128)(2,1)S(1)}, u32[]{:S(2)}, u32[]{:S(2)}) collective-permute-start(f16[2,192,128]{2,1,0:T(8,128)(2,1)S(1)} %bitcast.149), channel_id=1, source_target_pairs={{0,10},{2,8},{4,14},{6,12},{8,2},{10,0},{12,6},{14,4},{1,11},{3,9}... | collective-permute-start | bytes 294920 | tf_op jit(solution)/shard_map/ppermute | solution.py:737
  74.4 3.7 %rows_both_ways.3 = f32[8,2,192,128]{3,2,1,0:T(8,128)S(1)} custom-call(s32[2]{0:T(128)S(1)} %pad_add_fusion.first.token.place, f32[8,2,192,128]{3,2,1,0:T(8,128)S(1)} %convert_dynamic-update-slice_fusion.14.data, f32[8,96,128]{2,1,0:T(8,128)S(1)} %get-tuple-element.36.kept, f32[2,8,384,128]{3,2,1,0:T(8,128)S(1)} %get-tuple-element.37.target, ...), custom_call_target="tpu_custom_call" | custom-call | flops 603979776 | bytes 6291456 | tf_op jit(solution)/shard_map/rows_both_ways/pallas_call | solution.py:535
  78.1 0.2 convert.68
  78.3 0.2 slice_bitcast_fusion.2
  78.4 0.7 collective-permute-start.9
  79.2 3.2 %collective-permute-start.10 = (f16[2,192,128]{2,1,0:T(8,128)(2,1)S(1)}, f16[2,192,128]{2,1,0:T(8,128)(2,1)S(1)}, u32[]{:S(2)}, u32[]{:S(2)}) collective-permute-start(f16[2,192,128]{2,1,0:T(8,128)(2,1)S(1)} %bitcast.147), channel_id=1, source_target_pairs={{0,14},{2,12},{4,10},{6,8},{8,6},{10,4},{12,2},{14,0},{1,15},{3,13... | collective-permute-start | bytes 294920 | tf_op jit(solution)/shard_map/ppermute | solution.py:737
  82.4 1.6 %collective-permute-start.25 = (f16[2,192,128]{2,1,0:T(8,128)(2,1)S(1)}, f16[2,192,128]{2,1,0:T(8,128)(2,1)S(1)}, u32[]{:S(2)}, u32[]{:S(2)}) collective-permute-start(f16[2,192,128]{2,1,0:T(8,128)(2,1)S(1)} %get-tuple-element.63), channel_id=1, source_target_pairs={{0,2},{2,0},{4,6},{6,4},{8,10},{10,8},{12,14},{14,12},{1,3},{3,1},... | collective-permute-start | bytes 294920 | tf_op jit(solution)/shard_map/ppermute | solution.py:737
  84.0 0.1 collective-permute-start.26
  84.1 2.0 %collective-permute-start.27 = (f16[2,192,128]{2,1,0:T(8,128)(2,1)S(1)}, f16[2,192,128]{2,1,0:T(8,128)(2,1)S(1)}, u32[]{:S(2)}, u32[]{:S(2)}) collective-permute-start(f16[2,192,128]{2,1,0:T(8,128)(2,1)S(1)} %get-tuple-element.61), channel_id=1, source_target_pairs={{0,6},{2,4},{4,2},{6,0},{8,14},{10,12},{12,10},{14,8},{1,7},{3,5},... | collective-permute-start | bytes 294920 | tf_op jit(solution)/shard_map/ppermute | solution.py:737
  86.1 1.2 collective-permute-start.28
  87.4 0.6 collective-permute-done.10
  88.0 3.9 %rows_both_ways.2 = f32[8,2,192,128]{3,2,1,0:T(8,128)S(1)} custom-call(s32[2]{0:T(128)S(1)} %pad_add_fusion.first.token.place, f32[8,2,192,128]{3,2,1,0:T(8,128)S(1)} %convert_dynamic-update-slice_fusion.21.data, f32[8,96,128]{2,1,0:T(8,128)S(1)} %get-tuple-element.36.kept, f32[2,8,384,128]{3,2,1,0:T(8,128)S(1)} %get-tuple-element.37.target, ...), custom_call_target="tpu_custom_call" | custom-call | flops 603979776 | bytes 6291456 | tf_op jit(solution)/shard_map/rows_both_ways/pallas_call | solution.py:535
  91.9 0.2 convert.66
  92.1 0.2 slice_bitcast_fusion.9
  92.3 4.6 %collective-permute-start.29 = (f16[2,192,128]{2,1,0:T(8,128)(2,1)S(1)}, f16[2,192,128]{2,1,0:T(8,128)(2,1)S(1)}, u32[]{:S(2)}, u32[]{:S(2)}) collective-permute-start(f16[2,192,128]{2,1,0:T(8,128)(2,1)S(1)} %get-tuple-element.59), channel_id=1, source_target_pairs={{0,10},{2,8},{4,14},{6,12},{8,2},{10,0},{12,6},{14,4},{1,11},{3,9}... | collective-permute-start | bytes 294920 | tf_op jit(solution)/shard_map/ppermute | solution.py:737
  96.9 0.3 collective-permute-start.30
  97.2 3.2 %collective-permute-start.31 = (f16[2,192,128]{2,1,0:T(8,128)(2,1)S(1)}, f16[2,192,128]{2,1,0:T(8,128)(2,1)S(1)}, u32[]{:S(2)}, u32[]{:S(2)}) collective-permute-start(f16[2,192,128]{2,1,0:T(8,128)(2,1)S(1)} %get-tuple-element.57), channel_id=1, source_target_pairs={{0,14},{2,12},{4,10},{6,8},{8,6},{10,4},{12,2},{14,0},{1,15},{3,13... | collective-permute-start | bytes 294920 | tf_op jit(solution)/shard_map/ppermute | solution.py:737
  100.4 1.8 %collective-permute-start.11 = (f16[2,192,128]{2,1,0:T(8,128)(2,1)S(1)}, f16[2,192,128]{2,1,0:T(8,128)(2,1)S(1)}, u32[]{:S(2)}, u32[]{:S(2)}) collective-permute-start(f16[2,192,128]{2,1,0:T(8,128)(2,1)S(1)} %get-tuple-element.77), channel_id=1, source_target_pairs={{0,2},{2,0},{4,6},{6,4},{8,10},{10,8},{12,14},{14,12},{1,3},{3,1},... | collective-permute-start | bytes 294920 | tf_op jit(solution)/shard_map/ppermute | solution.py:737
  102.3 0.6 collective-permute-done.29
  102.8 1.2 collective-permute-start.13
  104.0 0.5 collective-permute-done.30
  104.4 4.1 %collective-permute-start.14 = (f16[2,192,128]{2,1,0:T(8,128)(2,1)S(1)}, f16[2,192,128]{2,1,0:T(8,128)(2,1)S(1)}, u32[]{:S(2)}, u32[]{:S(2)}) collective-permute-start(f16[2,192,128]{2,1,0:T(8,128)(2,1)S(1)} %get-tuple-element.74), channel_id=1, source_target_pairs={{0,8},{2,10},{4,12},{6,14},{8,0},{10,2},{12,4},{14,6},{1,9},{3,11}... | collective-permute-start | bytes 294920 | tf_op jit(solution)/shard_map/ppermute | solution.py:737
  108.5 6.6 %collective-permute-start.15 = (f16[2,192,128]{2,1,0:T(8,128)(2,1)S(1)}, f16[2,192,128]{2,1,0:T(8,128)(2,1)S(1)}, u32[]{:S(2)}, u32[]{:S(2)}) collective-permute-start(f16[2,192,128]{2,1,0:T(8,128)(2,1)S(1)} %get-tuple-element.73), channel_id=1, source_target_pairs={{0,10},{2,8},{4,14},{6,12},{8,2},{10,0},{12,6},{14,4},{1,11},{3,9}... | collective-permute-start | bytes 294920 | tf_op jit(solution)/shard_map/ppermute | solution.py:737
  115.4 4.0 %collective-permute-start.17 = (f16[2,192,128]{2,1,0:T(8,128)(2,1)S(1)}, f16[2,192,128]{2,1,0:T(8,128)(2,1)S(1)}, u32[]{:S(2)}, u32[]{:S(2)}) collective-permute-start(f16[2,192,128]{2,1,0:T(8,128)(2,1)S(1)} %get-tuple-element.71), channel_id=1, source_target_pairs={{0,14},{2,12},{4,10},{6,8},{8,6},{10,4},{12,2},{14,0},{1,15},{3,13... | collective-permute-start | bytes 294920 | tf_op jit(solution)/shard_map/ppermute | solution.py:737
  119.4 2.3 %columns_inverse.2.refs_0_ = f32[2,128,768]{2,1,0:T(8,128)S(1)} custom-call(s32[2]{0:T(128)S(1)} %pad_add_fusion.first.token.place, f32[8,2,2,3,32,128]{5,4,3,2,1,0:T(8,128)S(1)} %convert_dynamic-update-slice_fusion.7.data, f32[4,2,128,768]{3,2,1,0:T(8,128)S(1)} %copy-done.1, f32[8,128]{1,0:T(8,128)S(1)} %get-tuple-element.35.scales, ...), custom_call_target="tpu_custom_call" | custom-call | flops 1207959552 | bytes 3145728 | tf_op jit(solution)/shard_map/columns_inverse/pallas_call | solution.py:624
  121.8 1.4 %collective-permute-done.17 = f16[2,192,128]{2,1,0:T(8,128)(2,1)S(1)} collective-permute-done((f16[2,192,128]{2,1,0:T(8,128)(2,1)S(1)}, f16[2,192,128]{2,1,0:T(8,128)(2,1)S(1)}, u32[]{:S(2)}, u32[]{:S(2)}) %collective-permute-start.17) | collective-permute-done | bytes 98336 | tf_op jit(solution)/shard_map/ppermute | solution.py:737
  123.4 2.4 %columns_inverse.3 = (f32[2,128,384]{2,1,0:T(8,128)S(1)}, f32[2,128,384]{2,1,0:T(8,128)S(1)}) custom-call(s32[2]{0:T(128)S(1)} %pad_add_fusion.first.token.place, f32[8,2,2,3,32,128]{5,4,3,2,1,0:T(8,128)S(1)} %convert_dynamic-update-slice_fusion.data, f32[4,2,128,768]{3,2,1,0:T(8,128)S(1)} %copy-done.1, f32[8,128]{1,0:T(8,128)S(1)} %get-tuple-element.35.scales, ...), custom_call_target="tpu_custom_call" | custom-call | flops 1207959552 | bytes 3145728 | tf_op jit(solution)/shard_map/columns_inverse/pallas_call | solution.py:624
  125.9 1.7 %collective-permute-done.32 = f32[2,128,384]{2,1,0:T(8,128)S(1)} collective-permute-done((f32[2,128,384]{2,1,0:T(8,128)S(1)}, f32[2,128,384]{2,1,0:T(8,128)S(1)}, u32[]{:S(2)}, u32[]{:S(2)}) %collective-permute-start.32) | collective-permute-done | bytes 393248 | tf_op jit(solution)/shard_map/ppermute | solution.py:328
  127.6 0.9 multiply_add_fusion
  (97 shorter events, 0.9 us)
Async XLA Ops:
  1.1 1.5 %collective-permute-start = (f32[2,128,8]{2,1,0:T(8,128)S(1)}, f32[2,128,8]{2,1,0:T(8,128)S(1)}, u32[]{:S(2)}, u32[]{:S(2)}) collective-permute-start(f32[2,128,8]{2,1,0:T(8,128)S(1)} %slice_select_fusion), channel_id=1, source_target_pairs={{0,1},{1,0},{2,3},{3,2},{4,5},{5,4},{6,7},{7,6},{8,9},{9,8},{10,11... | collective-permute-start | bytes 24584 | tf_op jit(solution)/shard_map/ppermute | solution.py:328
  2.6 9.9 %collective-permute-start.1 = (f32[2,8,392]{2,1,0:T(8,128)S(1)}, f32[2,8,392]{2,1,0:T(8,128)S(1)}, u32[]{:S(2)}, u32[]{:S(2)}) collective-permute-start(f32[2,8,392]{2,1,0:T(8,128)S(1)} %pad_maximum_fusion), channel_id=1, source_target_pairs={{0,2},{2,4},{4,6},{6,8},{8,10},{10,12},{12,14},{1,3},{3,5},{5,7},{... | collective-permute-start | bytes 75272 | tf_op jit(solution)/shard_map/ppermute | solution.py:321
  7.4 5.8 %collective-permute-start.2 = (f32[2,8,392]{2,1,0:T(8,128)S(1)}, f32[2,8,392]{2,1,0:T(8,128)S(1)}, u32[]{:S(2)}, u32[]{:S(2)}) collective-permute-start(f32[2,8,392]{2,1,0:T(8,128)S(1)} %pad_maximum_fusion.1), channel_id=1, source_target_pairs={{2,0},{4,2},{6,4},{8,6},{10,8},{12,10},{14,12},{3,1},{5,3},{7,5},{... | collective-permute-start | bytes 75272 | tf_op jit(solution)/shard_map/ppermute | solution.py:322
  8.8 1.1 copy-start.8
  9.9 0.9 copy-start.10
  10.8 0.7 copy-start.13
  11.5 0.7 copy-start.14
  13.2 1.0 copy-start.9
  14.2 19.5 %copy-start = (f32[2,96,4,1024]{3,2,1,0:T(4,128)S(1)}, f32[2,96,4,1024]{3,2,1,0:T(4,128)}, u32[]{:S(2)}) copy-start(f32[2,96,4,1024]{3,2,1,0:T(4,128)} %refs_7_.1) | copy-start | bytes 9437188
  14.2 19.5 %copy-start.2 = (s32[96,1024]{1,0:T(8,128)S(1)}, s32[96,1024]{1,0:T(8,128)}, u32[]{:S(2)}) copy-start(s32[96,1024]{1,0:T(8,128)} %refs_15_.1) | copy-start | bytes 1179652
  33.6 5.1 %collective-permute-start.3 = (f32[2,128,384]{2,1,0:T(8,128)S(1)}, f32[2,128,384]{2,1,0:T(8,128)S(1)}, u32[]{:S(2)}, u32[]{:S(2)}) collective-permute-start(f32[2,128,384]{2,1,0:T(8,128)S(1)} %get-tuple-element.34.mine), channel_id=1, source_target_pairs={{0,1},{1,0},{2,3},{3,2},{4,5},{5,4},{6,7},{7,6},{8,9},{9,8},{10,11... | collective-permute-start | bytes 1179656 | tf_op jit(solution)/shard_map/ppermute | solution.py:328
  33.7 4.9 %copy-start.1 = (f32[4,2,128,768]{3,2,1,0:T(8,128)S(1)}, f32[4,2,128,768]{3,2,1,0:T(8,128)}, u32[]{:S(2)}) copy-start(f32[4,2,128,768]{3,2,1,0:T(8,128)} %maps.7) | copy-start | bytes 9437188
  33.7 4.9 %copy-start.3 = (bf16[2,512,512]{2,1,0:T(8,128)(2,1)S(1)}, bf16[2,512,512]{2,1,0:T(8,128)(2,1)}, u32[]{:S(2)}) copy-start(bf16[2,512,512]{2,1,0:T(8,128)(2,1)} %constant.33.clone.matrix) | copy-start | bytes 3145732
  33.7 4.9 %copy-start.11 = (f32[2,3,256]{2,1,0:T(4,128)S(1)}, f32[2,3,256]{2,1,0:T(4,128)}, u32[]{:S(2)}) copy-start(f32[2,3,256]{2,1,0:T(4,128)} %constant.34.clone.table) | copy-start | bytes 18436
  41.0 2.5 %copy-start.5 = (f32[8,2,2,3,32,128]{5,4,3,2,1,0:T(8,128)}, f32[8,2,2,3,32,128]{5,4,3,2,1,0:T(8,128)S(1)}, u32[]{:S(2)}) copy-start(f32[8,2,2,3,32,128]{5,4,3,2,1,0:T(8,128)S(1)} %columns_forward.3) | copy-start | bytes 4718596
  43.5 1.2 copy-start.4
  43.7 3.4 %slice-start.1 = ((f32[8,2,2,3,32,128]{5,4,3,2,1,0:T(8,128)}), f32[1,2,2,3,32,128]{5,4,3,2,1,0:T(8,128)S(1)}, s32[]{:S(2)}) async-start(f32[8,2,2,3,32,128]{5,4,3,2,1,0:T(8,128)} %copy-done.5), calls=%async_computation.1 | async-start | bytes 393216 | tf_op jit(solution)/shard_map/slice | solution.py:734
  44.7 8.6 %slice-start = ((f32[8,2,2,3,32,128]{5,4,3,2,1,0:T(8,128)}), f32[1,2,2,3,32,128]{5,4,3,2,1,0:T(8,128)S(1)}, s32[]{:S(2)}) async-start(f32[8,2,2,3,32,128]{5,4,3,2,1,0:T(8,128)} %copy-done.4), calls=%async_computation | async-start | bytes 393216 | tf_op jit(solution)/shard_map/slice | solution.py:734
  44.7 8.6 %collective-permute-start.18 = (f16[2,192,128]{2,1,0:T(8,128)(2,1)S(1)}, f16[2,192,128]{2,1,0:T(8,128)(2,1)S(1)}, u32[]{:S(2)}, u32[]{:S(2)}) collective-permute-start(f16[2,192,128]{2,1,0:T(8,128)(2,1)S(1)} %bitcast.160), channel_id=1, source_target_pairs={{0,2},{2,0},{4,6},{6,4},{8,10},{10,8},{12,14},{14,12},{1,3},{3,1},... | collective-permute-start | bytes 294920 | tf_op jit(solution)/shard_map/ppermute | solution.py:737
  47.2 9.4 %collective-permute-start.19 = (f16[2,192,128]{2,1,0:T(8,128)(2,1)S(1)}, f16[2,192,128]{2,1,0:T(8,128)(2,1)S(1)}, u32[]{:S(2)}, u32[]{:S(2)}) collective-permute-start(f16[2,192,128]{2,1,0:T(8,128)(2,1)S(1)} %bitcast.159), channel_id=1, source_target_pairs={{0,4},{2,6},{4,0},{6,2},{8,12},{10,14},{12,8},{14,10},{1,5},{3,7},... | collective-permute-start | bytes 294920 | tf_op jit(solution)/shard_map/ppermute | solution.py:737
  48.8 9.3 %collective-permute-start.20 = (f16[2,192,128]{2,1,0:T(8,128)(2,1)S(1)}, f16[2,192,128]{2,1,0:T(8,128)(2,1)S(1)}, u32[]{:S(2)}, u32[]{:S(2)}) collective-permute-start(f16[2,192,128]{2,1,0:T(8,128)(2,1)S(1)} %bitcast.158), channel_id=1, source_target_pairs={{0,6},{2,4},{4,2},{6,0},{8,14},{10,12},{12,10},{14,8},{1,7},{3,5},... | collective-permute-start | bytes 294920 | tf_op jit(solution)/shard_map/ppermute | solution.py:737
  49.3 9.7 %collective-permute-start.21 = (f16[2,192,128]{2,1,0:T(8,128)(2,1)S(1)}, f16[2,192,128]{2,1,0:T(8,128)(2,1)S(1)}, u32[]{:S(2)}, u32[]{:S(2)}) collective-permute-start(f16[2,192,128]{2,1,0:T(8,128)(2,1)S(1)} %bitcast.157), channel_id=1, source_target_pairs={{0,8},{2,10},{4,12},{6,14},{8,0},{10,2},{12,4},{14,6},{1,9},{3,11}... | collective-permute-start | bytes 294920 | tf_op jit(solution)/shard_map/ppermute | solution.py:737
  52.2 15.1 %collective-permute-start.22 = (f16[2,192,128]{2,1,0:T(8,128)(2,1)S(1)}, f16[2,192,128]{2,1,0:T(8,128)(2,1)S(1)}, u32[]{:S(2)}, u32[]{:S(2)}) collective-permute-start(f16[2,192,128]{2,1,0:T(8,128)(2,1)S(1)} %bitcast.156), channel_id=1, source_target_pairs={{0,10},{2,8},{4,14},{6,12},{8,2},{10,0},{12,6},{14,4},{1,11},{3,9}... | collective-permute-start | bytes 294920 | tf_op jit(solution)/shard_map/ppermute | solution.py:737
  53.3 21.1 %copy-start.6 = (bf16[2,256,256]{2,1,0:T(8,128)(2,1)S(1)}, bf16[2,256,256]{2,1,0:T(8,128)(2,1)}, u32[]{:S(2)}) copy-start(bf16[2,256,256]{2,1,0:T(8,128)(2,1)} %constant.35.clone.forward) | copy-start | bytes 786436
  53.3 21.1 %copy-start.7 = (bf16[2,256,256]{2,1,0:T(8,128)(2,1)S(1)}, bf16[2,256,256]{2,1,0:T(8,128)(2,1)}, u32[]{:S(2)}) copy-start(bf16[2,256,256]{2,1,0:T(8,128)(2,1)} %constant.36.clone.inverse) | copy-start | bytes 786436
  53.3 21.1 %copy-start.12 = (f32[2,8,128]{2,1,0:T(8,128)S(1)}, f32[2,8,128]{2,1,0:T(8,128)}, u32[]{:S(2)}) copy-start(f32[2,8,128]{2,1,0:T(8,128)} %constant.37.clone.table) | copy-start | bytes 24580
  53.4 14.0 %collective-permute-start.23 = (f16[2,192,128]{2,1,0:T(8,128)(2,1)S(1)}, f16[2,192,128]{2,1,0:T(8,128)(2,1)S(1)}, u32[]{:S(2)}, u32[]{:S(2)}) collective-permute-start(f16[2,192,128]{2,1,0:T(8,128)(2,1)S(1)} %bitcast.155), channel_id=1, source_target_pairs={{0,12},{2,14},{4,8},{6,10},{8,4},{10,6},{12,0},{14,2},{1,13},{3,15... | collective-permute-start | bytes 294920 | tf_op jit(solution)/shard_map/ppermute | solution.py:737
  56.6 14.9 %collective-permute-start.24 = (f16[2,192,128]{2,1,0:T(8,128)(2,1)S(1)}, f16[2,192,128]{2,1,0:T(8,128)(2,1)S(1)}, u32[]{:S(2)}, u32[]{:S(2)}) collective-permute-start(f16[2,192,128]{2,1,0:T(8,128)(2,1)S(1)} %bitcast.153), channel_id=1, source_target_pairs={{0,14},{2,12},{4,10},{6,8},{8,6},{10,4},{12,2},{14,0},{1,15},{3,13... | collective-permute-start | bytes 294920 | tf_op jit(solution)/shard_map/ppermute | solution.py:737
  58.1 20.3 %collective-permute-start.4 = (f16[2,192,128]{2,1,0:T(8,128)(2,1)S(1)}, f16[2,192,128]{2,1,0:T(8,128)(2,1)S(1)}, u32[]{:S(2)}, u32[]{:S(2)}) collective-permute-start(f16[2,192,128]{2,1,0:T(8,128)(2,1)S(1)} %bitcast.154), channel_id=1, source_target_pairs={{0,2},{2,0},{4,6},{6,4},{8,10},{10,8},{12,14},{14,12},{1,3},{3,1},... | collective-permute-start | bytes 294920 | tf_op jit(solution)/shard_map/ppermute | solution.py:737
  58.9 20.2 %collective-permute-start.5 = (f16[2,192,128]{2,1,0:T(8,128)(2,1)S(1)}, f16[2,192,128]{2,1,0:T(8,128)(2,1)S(1)}, u32[]{:S(2)}, u32[]{:S(2)}) collective-permute-start(f16[2,192,128]{2,1,0:T(8,128)(2,1)S(1)} %bitcast.152), channel_id=1, source_target_pairs={{0,4},{2,6},{4,0},{6,2},{8,12},{10,14},{12,8},{14,10},{1,5},{3,7},... | collective-permute-start | bytes 294920 | tf_op jit(solution)/shard_map/ppermute | solution.py:737
  67.3 15.0 %collective-permute-start.6 = (f16[2,192,128]{2,1,0:T(8,128)(2,1)S(1)}, f16[2,192,128]{2,1,0:T(8,128)(2,1)S(1)}, u32[]{:S(2)}, u32[]{:S(2)}) collective-permute-start(f16[2,192,128]{2,1,0:T(8,128)(2,1)S(1)} %bitcast.151), channel_id=1, source_target_pairs={{0,6},{2,4},{4,2},{6,0},{8,14},{10,12},{12,10},{14,8},{1,7},{3,5},... | collective-permute-start | bytes 294920 | tf_op jit(solution)/shard_map/ppermute | solution.py:737
  67.4 16.6 %collective-permute-start.7 = (f16[2,192,128]{2,1,0:T(8,128)(2,1)S(1)}, f16[2,192,128]{2,1,0:T(8,128)(2,1)S(1)}, u32[]{:S(2)}, u32[]{:S(2)}) collective-permute-start(f16[2,192,128]{2,1,0:T(8,128)(2,1)S(1)} %bitcast.150), channel_id=1, source_target_pairs={{0,8},{2,10},{4,12},{6,14},{8,0},{10,2},{12,4},{14,6},{1,9},{3,11}... | collective-permute-start | bytes 294920 | tf_op jit(solution)/shard_map/ppermute | solution.py:737
  71.5 12.6 %collective-permute-start.8 = (f16[2,192,128]{2,1,0:T(8,128)(2,1)S(1)}, f16[2,192,128]{2,1,0:T(8,128)(2,1)S(1)}, u32[]{:S(2)}, u32[]{:S(2)}) collective-permute-start(f16[2,192,128]{2,1,0:T(8,128)(2,1)S(1)} %bitcast.149), channel_id=1, source_target_pairs={{0,10},{2,8},{4,14},{6,12},{8,2},{10,0},{12,6},{14,4},{1,11},{3,9}... | collective-permute-start | bytes 294920 | tf_op jit(solution)/shard_map/ppermute | solution.py:737
  78.4 7.7 %collective-permute-start.9 = (f16[2,192,128]{2,1,0:T(8,128)(2,1)S(1)}, f16[2,192,128]{2,1,0:T(8,128)(2,1)S(1)}, u32[]{:S(2)}, u32[]{:S(2)}) collective-permute-start(f16[2,192,128]{2,1,0:T(8,128)(2,1)S(1)} %bitcast.148), channel_id=1, source_target_pairs={{0,12},{2,14},{4,8},{6,10},{8,4},{10,6},{12,0},{14,2},{1,13},{3,15... | collective-permute-start | bytes 294920 | tf_op jit(solution)/shard_map/ppermute | solution.py:737
  79.2 8.8 %collective-permute-start.10 = (f16[2,192,128]{2,1,0:T(8,128)(2,1)S(1)}, f16[2,192,128]{2,1,0:T(8,128)(2,1)S(1)}, u32[]{:S(2)}, u32[]{:S(2)}) collective-permute-start(f16[2,192,128]{2,1,0:T(8,128)(2,1)S(1)} %bitcast.147), channel_id=1, source_target_pairs={{0,14},{2,12},{4,10},{6,8},{8,6},{10,4},{12,2},{14,0},{1,15},{3,13... | collective-permute-start | bytes 294920 | tf_op jit(solution)/shard_map/ppermute | solution.py:737
  82.4 14.5 %collective-permute-start.25 = (f16[2,192,128]{2,1,0:T(8,128)(2,1)S(1)}, f16[2,192,128]{2,1,0:T(8,128)(2,1)S(1)}, u32[]{:S(2)}, u32[]{:S(2)}) collective-permute-start(f16[2,192,128]{2,1,0:T(8,128)(2,1)S(1)} %get-tuple-element.63), channel_id=1, source_target_pairs={{0,2},{2,0},{4,6},{6,4},{8,10},{10,8},{12,14},{14,12},{1,3},{3,1},... | collective-permute-start | bytes 294920 | tf_op jit(solution)/shard_map/ppermute | solution.py:737
  84.0 13.2 %collective-permute-start.26 = (f16[2,192,128]{2,1,0:T(8,128)(2,1)S(1)}, f16[2,192,128]{2,1,0:T(8,128)(2,1)S(1)}, u32[]{:S(2)}, u32[]{:S(2)}) collective-permute-start(f16[2,192,128]{2,1,0:T(8,128)(2,1)S(1)} %get-tuple-element.62), channel_id=1, source_target_pairs={{0,4},{2,6},{4,0},{6,2},{8,12},{10,14},{12,8},{14,10},{1,5},{3,7},... | collective-permute-start | bytes 294920 | tf_op jit(solution)/shard_map/ppermute | solution.py:737
  84.1 16.3 %collective-permute-start.27 = (f16[2,192,128]{2,1,0:T(8,128)(2,1)S(1)}, f16[2,192,128]{2,1,0:T(8,128)(2,1)S(1)}, u32[]{:S(2)}, u32[]{:S(2)}) collective-permute-start(f16[2,192,128]{2,1,0:T(8,128)(2,1)S(1)} %get-tuple-element.61), channel_id=1, source_target_pairs={{0,6},{2,4},{4,2},{6,0},{8,14},{10,12},{12,10},{14,8},{1,7},{3,5},... | collective-permute-start | bytes 294920 | tf_op jit(solution)/shard_map/ppermute | solution.py:737
  86.1 16.1 %collective-permute-start.28 = (f16[2,192,128]{2,1,0:T(8,128)(2,1)S(1)}, f16[2,192,128]{2,1,0:T(8,128)(2,1)S(1)}, u32[]{:S(2)}, u32[]{:S(2)}) collective-permute-start(f16[2,192,128]{2,1,0:T(8,128)(2,1)S(1)} %get-tuple-element.60), channel_id=1, source_target_pairs={{0,8},{2,10},{4,12},{6,14},{8,0},{10,2},{12,4},{14,6},{1,9},{3,11}... | collective-permute-start | bytes 294920 | tf_op jit(solution)/shard_map/ppermute | solution.py:737
  92.3 10.6 %collective-permute-start.29 = (f16[2,192,128]{2,1,0:T(8,128)(2,1)S(1)}, f16[2,192,128]{2,1,0:T(8,128)(2,1)S(1)}, u32[]{:S(2)}, u32[]{:S(2)}) collective-permute-start(f16[2,192,128]{2,1,0:T(8,128)(2,1)S(1)} %get-tuple-element.59), channel_id=1, source_target_pairs={{0,10},{2,8},{4,14},{6,12},{8,2},{10,0},{12,6},{14,4},{1,11},{3,9}... | collective-permute-start | bytes 294920 | tf_op jit(solution)/shard_map/ppermute | solution.py:737
  96.9 7.6 %collective-permute-start.30 = (f16[2,192,128]{2,1,0:T(8,128)(2,1)S(1)}, f16[2,192,128]{2,1,0:T(8,128)(2,1)S(1)}, u32[]{:S(2)}, u32[]{:S(2)}) collective-permute-start(f16[2,192,128]{2,1,0:T(8,128)(2,1)S(1)} %get-tuple-element.58), channel_id=1, source_target_pairs={{0,12},{2,14},{4,8},{6,10},{8,4},{10,6},{12,0},{14,2},{1,13},{3,15... | collective-permute-start | bytes 294920 | tf_op jit(solution)/shard_map/ppermute | solution.py:737
  97.2 11.3 %collective-permute-start.31 = (f16[2,192,128]{2,1,0:T(8,128)(2,1)S(1)}, f16[2,192,128]{2,1,0:T(8,128)(2,1)S(1)}, u32[]{:S(2)}, u32[]{:S(2)}) collective-permute-start(f16[2,192,128]{2,1,0:T(8,128)(2,1)S(1)} %get-tuple-element.57), channel_id=1, source_target_pairs={{0,14},{2,12},{4,10},{6,8},{8,6},{10,4},{12,2},{14,0},{1,15},{3,13... | collective-permute-start | bytes 294920 | tf_op jit(solution)/shard_map/ppermute | solution.py:737
  100.4 14.9 %collective-permute-start.11 = (f16[2,192,128]{2,1,0:T(8,128)(2,1)S(1)}, f16[2,192,128]{2,1,0:T(8,128)(2,1)S(1)}, u32[]{:S(2)}, u32[]{:S(2)}) collective-permute-start(f16[2,192,128]{2,1,0:T(8,128)(2,1)S(1)} %get-tuple-element.77), channel_id=1, source_target_pairs={{0,2},{2,0},{4,6},{6,4},{8,10},{10,8},{12,14},{14,12},{1,3},{3,1},... | collective-permute-start | bytes 294920 | tf_op jit(solution)/shard_map/ppermute | solution.py:737
  102.3 13.1 %collective-permute-start.12 = (f16[2,192,128]{2,1,0:T(8,128)(2,1)S(1)}, f16[2,192,128]{2,1,0:T(8,128)(2,1)S(1)}, u32[]{:S(2)}, u32[]{:S(2)}) collective-permute-start(f16[2,192,128]{2,1,0:T(8,128)(2,1)S(1)} %get-tuple-element.76), channel_id=1, source_target_pairs={{0,4},{2,6},{4,0},{6,2},{8,12},{10,14},{12,8},{14,10},{1,5},{3,7},... | collective-permute-start | bytes 294920 | tf_op jit(solution)/shard_map/ppermute | solution.py:737
  102.8 18.9 %collective-permute-start.13 = (f16[2,192,128]{2,1,0:T(8,128)(2,1)S(1)}, f16[2,192,128]{2,1,0:T(8,128)(2,1)S(1)}, u32[]{:S(2)}, u32[]{:S(2)}) collective-permute-start(f16[2,192,128]{2,1,0:T(8,128)(2,1)S(1)} %get-tuple-element.75), channel_id=1, source_target_pairs={{0,6},{2,4},{4,2},{6,0},{8,14},{10,12},{12,10},{14,8},{1,7},{3,5},... | collective-permute-start | bytes 294920 | tf_op jit(solution)/shard_map/ppermute | solution.py:737
  104.4 17.3 %collective-permute-start.14 = (f16[2,192,128]{2,1,0:T(8,128)(2,1)S(1)}, f16[2,192,128]{2,1,0:T(8,128)(2,1)S(1)}, u32[]{:S(2)}, u32[]{:S(2)}) collective-permute-start(f16[2,192,128]{2,1,0:T(8,128)(2,1)S(1)} %get-tuple-element.74), channel_id=1, source_target_pairs={{0,8},{2,10},{4,12},{6,14},{8,0},{10,2},{12,4},{14,6},{1,9},{3,11}... | collective-permute-start | bytes 294920 | tf_op jit(solution)/shard_map/ppermute | solution.py:737
  108.5 13.3 %collective-permute-start.15 = (f16[2,192,128]{2,1,0:T(8,128)(2,1)S(1)}, f16[2,192,128]{2,1,0:T(8,128)(2,1)S(1)}, u32[]{:S(2)}, u32[]{:S(2)}) collective-permute-start(f16[2,192,128]{2,1,0:T(8,128)(2,1)S(1)} %get-tuple-element.73), channel_id=1, source_target_pairs={{0,10},{2,8},{4,14},{6,12},{8,2},{10,0},{12,6},{14,4},{1,11},{3,9}... | collective-permute-start | bytes 294920 | tf_op jit(solution)/shard_map/ppermute | solution.py:737
  115.3 6.5 %collective-permute-start.16 = (f16[2,192,128]{2,1,0:T(8,128)(2,1)S(1)}, f16[2,192,128]{2,1,0:T(8,128)(2,1)S(1)}, u32[]{:S(2)}, u32[]{:S(2)}) collective-permute-start(f16[2,192,128]{2,1,0:T(8,128)(2,1)S(1)} %get-tuple-element.72), channel_id=1, source_target_pairs={{0,12},{2,14},{4,8},{6,10},{8,4},{10,6},{12,0},{14,2},{1,13},{3,15... | collective-permute-start | bytes 294920 | tf_op jit(solution)/shard_map/ppermute | solution.py:737
  115.4 7.8 %collective-permute-start.17 = (f16[2,192,128]{2,1,0:T(8,128)(2,1)S(1)}, f16[2,192,128]{2,1,0:T(8,128)(2,1)S(1)}, u32[]{:S(2)}, u32[]{:S(2)}) collective-permute-start(f16[2,192,128]{2,1,0:T(8,128)(2,1)S(1)} %get-tuple-element.71), channel_id=1, source_target_pairs={{0,14},{2,12},{4,10},{6,8},{8,6},{10,4},{12,2},{14,0},{1,15},{3,13... | collective-permute-start | bytes 294920 | tf_op jit(solution)/shard_map/ppermute | solution.py:737
  123.4 4.2 %copy-start.15 = (f32[2,128,384]{2,1,0:T(8,128)S(1)}, f32[2,128,384]{2,1,0:T(8,128)}, u32[]{:S(2)}) copy-start(f32[2,128,384]{2,1,0:T(8,128)} %param.24) | copy-start | bytes 1179652
  125.8 1.8 %collective-permute-start.32 = (f32[2,128,384]{2,1,0:T(8,128)S(1)}, f32[2,128,384]{2,1,0:T(8,128)S(1)}, u32[]{:S(2)}, u32[]{:S(2)}) collective-permute-start(f32[2,128,384]{2,1,0:T(8,128)S(1)} %get-tuple-element.55), channel_id=1, source_target_pairs={{0,1},{1,0},{2,3},{3,2},{4,5},{5,4},{6,7},{7,6},{8,9},{9,8},{10,11... | collective-permute-start | bytes 1179656 | tf_op jit(solution)/shard_map/ppermute | solution.py:328
